TPU v7x, 32 devices: a whole 2x2x4 slice. The times are simulated.
32 devices in a mesh: dp: 8 (over z, x), tensor: 4 (over y, core).
Axes of the slice: x: 2, y: 2, z: 4, core: 2. Of those that a mesh axis runs over, the one named last changes fastest.
Arguments:
- tokens: bfloat16 [20480, 768], P(('dp', 'tensor')), may hold values from -6 to 6
- lengths: int32 [8, 5], P('dp'), may hold values from 1 to 32, 40 in all within a row
- in_gain: float32 [768], replicated, may hold values from 0.25 to 1.75
- qkv_weight: bfloat16 [768, 2304], P(None, 'tensor'), may hold values from -0.21875 to 0.21875
- attn_gain: float32 [768], P('tensor'), may hold values from 0.25 to 1.75
- out_weight: bfloat16 [768, 768], P('tensor'), may hold values from -0.21875 to 0.21875
- ffn_gain: float32 [768], replicated, may hold values from 0.25 to 1.75
- up_weight: bfloat16 [768, 3072], P(None, 'tensor'), may hold values from -0.21875 to 0.21875
- hidden_gain: float32 [3072], P('tensor'), may hold values from 0.25 to 1.75
- down_weight: bfloat16 [3072, 768], P('tensor'), may hold values from -0.109375 to 0.109375
- out_grad: bfloat16 [20480, 768], P(('dp', 'tensor')), may hold values from -6 to 6
Outputs:
- output: bfloat16 [20480, 768], P(('dp', 'tensor'))
- in_grad: float32 [20480, 768], P(('dp', 'tensor'))
- grad_in_gain: float32 [768], replicated
- grad_qkv: float32 [768, 2304], P(None, 'tensor')
- grad_attn_gain: float32 [768], P('tensor')
- grad_out: float32 [768, 768], P('tensor')
- grad_ffn_gain: float32 [768], replicated
- grad_up: float32 [768, 3072], P(None, 'tensor')
- grad_hidden_gain: float32 [3072], P('tensor')
- grad_down: float32 [3072, 768], P('tensor')
Inputs may be any that keep to these rules, and one draw needn't show every extreme that they name: Each row of lengths sums to 40, and its largest entry is exactly 32.
All inputs are finite; a program needn't handle non-finite values.
Results may differ from a plain program's by a relative error of at most 0.015.
Values may be sent and summed in bfloat16 or wider, within the bound.
A program may use at most 192 MiB of HBM per device.

v0:
```python
from functools import partial

import jax
import jax.numpy as jnp
from jax import lax
from jax.sharding import PartitionSpec as P

D = 768
HEAD_DIM = 64
FF = 3072
UNIT = 64
MAXLEN = 2048
QB = 512


EPS = 1e-05


def contract_rows(left, right):
    return lax.dot_general(
        left, right, (((0,), (0,)), ((), ())), preferred_element_type=jnp.float32
    )


def contract_cols(left, right):
    return lax.dot_general(
        left, right, (((1,), (1,)), ((), ())), preferred_element_type=jnp.float32
    )


def normalize(values, gain):
    row_mean = jnp.mean(values, axis=1, keepdims=True)
    row_square = jnp.mean(values * values, axis=1, keepdims=True)
    inv_scale = lax.rsqrt(row_square - row_mean * row_mean + EPS)
    unit_rows = (values - row_mean) * inv_scale
    return (unit_rows, inv_scale, unit_rows * gain)


def norm_back(grad_normed, unit_rows, inv_scale, gain):
    weighted = grad_normed * gain
    first_mean = jnp.mean(weighted, axis=1, keepdims=True)
    second = jnp.mean(weighted * unit_rows, axis=1, keepdims=True)
    return (
        inv_scale * (weighted - first_mean - unit_rows * second),
        jnp.sum(grad_normed * unit_rows, axis=0),
    )


def segment_ids(counts, row_count):
    ends = jnp.cumsum(counts * UNIT)
    positions = jnp.arange(row_count, dtype=jnp.int32)
    return jnp.sum((positions[:, None] >= ends[None, :]).astype(jnp.int32), axis=1)


def split_heads(packed):
    row_count = packed.shape[0]
    head_count = packed.shape[1] // (3 * HEAD_DIM)
    heads_view = packed.reshape(row_count, head_count, 3, HEAD_DIM)
    return (heads_view[:, :, 0], heads_view[:, :, 1], heads_view[:, :, 2])


def block_scores(queries, keys, segment, block_index):
    row_count = queries.shape[0]
    width = MAXLEN + QB
    first_row = block_index * QB
    key_start = jnp.clip(first_row + QB - width, 0, row_count - width)
    query_block = lax.dynamic_slice_in_dim(queries, first_row, QB, 0)
    query_segment = lax.dynamic_slice_in_dim(segment, first_row, QB, 0)
    query_pos = first_row + jnp.arange(QB, dtype=jnp.int32)
    key_pos = key_start + jnp.arange(width, dtype=jnp.int32)
    allowed = (query_segment[:, None] == segment[None, :]) & (
        key_pos[None, :] <= query_pos[:, None]
    )
    score = jnp.einsum("qhe,khe->hqk", query_block, keys, preferred_element_type=jnp.float32) * (
        1.0 / float(HEAD_DIM) ** 0.5
    )
    return (jnp.where(allowed[None], score, -1000000000.0), query_block, keys, key_start)


def attention_forward(packed, segment):
    queries, keys, values = split_heads(packed)

    def one_block(block_index):
        score, query_block, key_window, key_start = block_scores(
            queries, keys, segment, block_index
        )
        top_score = jnp.max(score, axis=2, keepdims=True)
        exponent = jnp.exp(score - top_score)
        row_total = jnp.sum(exponent, axis=2, keepdims=True)
        weights = (exponent / row_total).astype(jnp.bfloat16)
        mixed = jnp.einsum("hqk,khe->qhe", weights, values, preferred_element_type=jnp.float32)
        return (mixed, (top_score + jnp.log(row_total))[:, :, 0])

    mixed, log_total = lax.map(one_block, jnp.arange(packed.shape[0] // QB, dtype=jnp.int32))
    return (mixed.reshape(packed.shape[0], -1), log_total)


def attention_backward(packed, segment, log_total, grad_mixed):
    queries, keys, values = split_heads(packed)
    row_count = packed.shape[0]
    head_count = queries.shape[1]
    grad_heads = grad_mixed.reshape(row_count, head_count, HEAD_DIM)
    scale = 1.0 / float(HEAD_DIM) ** 0.5

    def one_block(carry, block_index):
        grad_keys, grad_values = carry
        score, query_block, key_window, key_start = block_scores(
            queries, keys, segment, block_index
        )
        grad_block = lax.dynamic_slice_in_dim(grad_heads, block_index * QB, QB, 0)
        weights = jnp.exp(score - log_total[block_index][:, :, None])
        grad_weights = jnp.einsum(
            "qhe,khe->hqk", grad_block, values, preferred_element_type=jnp.float32
        )
        grad_score = (
            weights * (grad_weights - jnp.sum(weights * grad_weights, axis=2, keepdims=True))
        ).astype(jnp.bfloat16)
        grad_query = (
            jnp.einsum("hqk,khe->qhe", grad_score, key_window, preferred_element_type=jnp.float32)
            * scale
        )
        grad_key = (
            jnp.einsum("hqk,qhe->khe", grad_score, query_block, preferred_element_type=jnp.float32)
            * scale
        )
        grad_value = jnp.einsum(
            "hqk,qhe->khe",
            weights.astype(jnp.bfloat16),
            grad_block,
            preferred_element_type=jnp.float32,
        )
        grad_keys = grad_keys + grad_key
        grad_values = grad_values + grad_value
        return ((grad_keys, grad_values), grad_query)

    zeros = jnp.zeros((row_count, head_count, HEAD_DIM), jnp.float32)
    (grad_keys, grad_values), grad_queries = lax.scan(
        one_block, (zeros, zeros), jnp.arange(row_count // QB, dtype=jnp.int32)
    )
    grad_queries = grad_queries.reshape(row_count, head_count, HEAD_DIM)
    stacked = jnp.stack((grad_queries, grad_keys, grad_values), axis=2)
    return stacked.reshape(row_count, 3 * head_count * HEAD_DIM).astype(jnp.bfloat16)


def ffn_totals(grad_up, grad_down, grad_hidden):
    return lax.psum((grad_up, grad_down, grad_hidden), "dp")


def local(
    tokens,
    lengths,
    in_gain,
    qkv_weight,
    attn_gain,
    out_weight,
    ffn_gain,
    up_weight,
    hidden_gain,
    down_weight,
    out_grad,
):
    tensor_size = lax.axis_size("tensor")
    own_rows = tokens.shape[0]
    group_rows = own_rows * tensor_size
    segment = segment_ids(lengths[0], group_rows)
    residual = tokens.astype(jnp.float32)
    in_unit, in_scale, in_normed = normalize(residual, in_gain)
    gathered_in, gathered_grad = (
        lax.all_gather(in_normed.astype(jnp.bfloat16), "tensor", axis=0, tiled=True),
        lax.all_gather(out_grad, "tensor", axis=0, tiled=True),
    )
    packed = jnp.dot(gathered_in, qkv_weight, preferred_element_type=jnp.float32).astype(
        jnp.bfloat16
    )
    attended, log_total = attention_forward(packed, segment)
    att_sum, att_square = lax.psum(
        (jnp.sum(attended, axis=1), jnp.sum(attended * attended, axis=1)), "tensor"
    )
    att_mean = att_sum / D
    att_scale = lax.rsqrt(att_square / D - att_mean * att_mean + EPS)
    att_unit = (attended - att_mean[:, None]) * att_scale[:, None]
    att_low = (att_unit * attn_gain).astype(jnp.bfloat16)
    middle = residual + lax.psum_scatter(
        jnp.dot(att_low, out_weight, preferred_element_type=jnp.float32),
        "tensor",
        scatter_dimension=0,
        tiled=True,
    )
    mid_unit, mid_scale, mid_normed = normalize(middle, ffn_gain)
    mid_low = mid_normed.astype(jnp.bfloat16)
    gathered_mid = lax.all_gather(mid_low, "tensor", axis=0, tiled=True)
    pre_act = jnp.dot(gathered_mid, up_weight, preferred_element_type=jnp.float32)
    activated, gelu_pull = jax.vjp(partial(jax.nn.gelu, approximate=True), pre_act)
    act_sum, act_square = lax.psum(
        (jnp.sum(activated, axis=1), jnp.sum(activated * activated, axis=1)), "tensor"
    )
    act_mean = act_sum / FF
    act_scale = lax.rsqrt(act_square / FF - act_mean * act_mean + EPS)
    act_unit = (activated - act_mean[:, None]) * act_scale[:, None]
    act_low = (act_unit * hidden_gain).astype(jnp.bfloat16)
    result = (
        middle
        + lax.psum_scatter(
            jnp.dot(
                lax.slice_in_dim(act_low, 0, lax.axis_size("tensor") * own_rows, axis=0),
                down_weight,
                preferred_element_type=jnp.float32,
            ).astype(jnp.bfloat16),
            "tensor",
            scatter_dimension=0,
            tiled=True,
        ).astype(jnp.float32)
    ).astype(jnp.bfloat16)
    grad_down = contract_rows(act_low, gathered_grad)
    grad_act_low = contract_cols(gathered_grad, down_weight)
    weighted_act = grad_act_low * hidden_gain
    grad_hidden = jnp.sum(grad_act_low * act_unit, axis=0)
    first_sum, second_sum = lax.psum(
        (jnp.sum(weighted_act, axis=1), jnp.sum(weighted_act * act_unit, axis=1)), "tensor"
    )
    grad_act = act_scale[:, None] * (
        weighted_act - (first_sum / FF)[:, None] - act_unit * (second_sum / FF)[:, None]
    )
    grad_pre = gelu_pull(grad_act)[0].astype(jnp.bfloat16)
    grad_up = contract_rows(gathered_mid, grad_pre)
    grad_mid_normed = lax.psum_scatter(
        contract_cols(grad_pre, up_weight), "tensor", scatter_dimension=0, tiled=True
    )
    grad_mid_part, grad_ffn_gain_part = norm_back(grad_mid_normed, mid_unit, mid_scale, ffn_gain)
    grad_middle = out_grad.astype(jnp.float32) + grad_mid_part
    gathered_back = lax.all_gather(grad_middle.astype(jnp.bfloat16), "tensor", axis=0, tiled=True)
    grad_out_part = contract_rows(att_low, gathered_back)
    grad_att_low = contract_cols(gathered_back, out_weight)
    weighted_att = grad_att_low * attn_gain
    grad_attn_gain_part = jnp.sum(grad_att_low * att_unit, axis=0)
    first_att, second_att, grad_ffn_gain_group = lax.psum(
        (
            jnp.sum(weighted_att, axis=1),
            jnp.sum(weighted_att * att_unit, axis=1),
            grad_ffn_gain_part,
        ),
        "tensor",
    )
    grad_attended = (
        att_scale[:, None]
        * (weighted_att - (first_att / D)[:, None] - att_unit * (second_att / D)[:, None])
    ).astype(jnp.bfloat16)
    grad_packed = attention_backward(packed, segment, log_total, grad_attended)
    grad_qkv_part = contract_rows(gathered_in, grad_packed)
    grad_in_normed = lax.psum_scatter(
        contract_cols(grad_packed, qkv_weight).astype(jnp.bfloat16),
        "tensor",
        scatter_dimension=0,
        tiled=True,
    ).astype(jnp.float32)
    grad_in_part, grad_in_gain_part = norm_back(grad_in_normed, in_unit, in_scale, in_gain)
    in_grad = grad_middle + grad_in_part
    ffn_sums = ffn_totals(grad_up, grad_down, grad_hidden)
    attn_sums = lax.psum(
        (grad_qkv_part, grad_out_part, grad_attn_gain_part, grad_ffn_gain_group), "dp"
    )
    grad_in_gain = lax.psum(grad_in_gain_part, ("dp", "tensor"))
    return (
        result,
        in_grad,
        grad_in_gain,
        attn_sums[0],
        attn_sums[2],
        attn_sums[1],
        attn_sums[3],
        ffn_sums[0],
        ffn_sums[2],
        ffn_sums[1],
    )


def solution(mesh):
    return jax.shard_map(
        local,
        mesh=mesh,
        in_specs=(
            P(("dp", "tensor"), None),
            P("dp", None),
            P(),
            P(None, "tensor"),
            P("tensor"),
            P("tensor", None),
            P(),
            P(None, "tensor"),
            P("tensor"),
            P("tensor", None),
            P(("dp", "tensor"), None),
        ),
        out_specs=(
            P(("dp", "tensor"), None),
            P(("dp", "tensor"), None),
            P(),
            P(None, "tensor"),
            P("tensor"),
            P("tensor", None),
            P(),
            P(None, "tensor"),
            P("tensor"),
            P("tensor", None),
        ),
        check_vma=False,
    )
```

profile of v0, /device:TPU:0, one launch (start us, length us, event | category | flops | bytes accessed | tf_op | source)
XLA Modules:
  0.0 1069.0 jit_solution(10255148810879272823)
XLA Ops:
  11.9 35.5 %all-gather.5.cloned.1.call-done = bf16[2560,768]{1,0:T(8,128)(2,1)} async-done(((bf16[640,768]{1,0:T(8,128)(2,1)}), bf16[2560,768]{1,0:T(8,128)(2,1)}) %all-gather.5.cloned.1.call-update) | async-done | bytes 3932176 | tf_op jit(solution)/shard_map/all_gather | solution.py:169
  53.2 82.3 %while.37 = (s32[]{:T(128)}, f32[5,512,3,64]{1,3,2,0:T(8,128)}, f32[5,3,512]{2,1,0:T(4,128)S(1)}, s32[5]{0:T(128)S(1)}, s32[2560]{0:T(1024)S(1)}, /*index=5*/bf1...) while((s32[]{:T(128)}, f32[5,512,3,64]{1,3,2,0:T(8,128)}, ...), condition=%wide.region_7.8_spmd.clone, body=%wide.region_4.7_spmd.sunk.clone | while | flops 1057752576 | bytes 55081176 | solution.py:94
  80.7 5.4 fusion.128
  97.2 5.4 fusion.128
  113.7 5.4 fusion.128
  146.6 10.7 all-reduce.5
  157.3 6.0 fusion.52
  163.4 70.2 %reduce-scatter.5.cloned.1.call-done = f32[640,768]{1,0:T(8,128)} async-done(((f32[2560,768]{1,0:T(8,128)}), f32[640,768]{1,0:T(8,128)}) %reduce-scatter.5.cloned.1.call-update) | async-done | bytes 1966096 | tf_op jit(solution)/shard_map/reduce_scatter | solution.py:183
  238.9 32.5 %all-gather.7.cloned.1.call-done = bf16[2560,768]{1,0:T(8,128)(2,1)} async-done(((bf16[640,768]{1,0:T(8,128)(2,1)}), bf16[2560,768]{1,0:T(8,128)(2,1)}) %all-gather.7.cloned.1.call-update) | async-done | bytes 3932176 | tf_op jit(solution)/shard_map/all_gather | solution.py:191
  271.4 9.5 fusion.54
  280.9 11.6 %all-reduce.4 = (f32[2560]{0:T(1024)S(1)}, f32[2560]{0:T(1024)S(1)}) all-reduce(f32[2560]{0:T(1024)S(1)} %get-tuple-element.435, f32[2560]{0:T(1024)S(1)} %get-tuple-element.434), channel_id=1, replica_groups=mesh['dp'=8,'tensor'=4] {'tensor'}, use_global_device_ids=true, to_apply=%region_18.19 | all-reduce | flops 5120 | bytes 40960 | tf_op jit(solution)/shard_map/psum | solution.py:194
  292.6 13.9 %all-gather.9.cloned.1.call-done = bf16[2560,768]{1,0:T(8,128)(2,1)} async-done(((bf16[640,768]{1,0:T(8,128)(2,1)}), bf16[2560,768]{1,0:T(8,128)(2,1)}) %all-gather.9.cloned.1.call-update) | async-done | bytes 3932176 | tf_op jit(solution)/shard_map/all_gather | solution.py:170
  306.5 11.7 %multiply_reduce_fusion.1 = (f32[768]{0:T(1024)}, f32[2560]{0:T(1024)S(1)}, f32[2560]{0:T(1024)S(1)}, f32[2560,768]{0,1:T(8,128)}) fusion(f32[2560]{0:T(1024)S(1)} %get-tuple-element.517, f32[2560]{0:T(1024)S(1)} %get-tuple-element.516, f32[2560,768]{0,1:T(8,128)} %get-tuple-element.524, f32[768]{0:T(1024)S(1)} %copy-done.33, ...), kind=kOutput, calls=%fused_computation.52 | convolution fusion | flops 3051350272 | bytes 20887552 | tf_op jit(solution)/shard_map/dot_general | solution.py:26
  318.2 10.9 %all-reduce.3 = (f32[2560]{0:T(1024)S(1)}, f32[2560]{0:T(1024)S(1)}) all-reduce(f32[2560]{0:T(1024)S(1)} %get-tuple-element.432, f32[2560]{0:T(1024)S(1)} %get-tuple-element.433), channel_id=1, replica_groups=mesh['dp'=8,'tensor'=4] {'tensor'}, use_global_device_ids=true, to_apply=%region_23.24 | all-reduce | flops 5120 | bytes 40960 | tf_op jit(solution)/shard_map/psum | solution.py:218
  329.0 10.2 fusion.37
  341.2 5.4 fusion.58
  346.7 8.7 convolution_convert_fusion
  355.5 61.3 %reduce-scatter.9.cloned.1.call-done = f32[640,768]{1,0:T(8,128)} async-done(((f32[2560,768]{1,0:T(8,128)}), f32[640,768]{1,0:T(8,128)}) %reduce-scatter.9.cloned.1.call-update) | async-done | bytes 1966096 | tf_op jit(solution)/shard_map/reduce_scatter | solution.py:226
  419.8 42.4 %reduce-scatter.7.cloned.1.call-done = bf16[640,768]{1,0:T(8,128)(2,1)} async-done(((bf16[2560,768]{1,0:T(8,128)(2,1)}), bf16[640,768]{1,0:T(8,128)(2,1)}) %reduce-scatter.7.cloned.1.call-update) | async-done | bytes 983056 | tf_op jit(solution)/shard_map/reduce_scatter | solution.py:203
  467.5 32.0 %all-gather.11.cloned.1.call-done = bf16[2560,768]{1,0:T(8,128)(2,1)} async-done(((bf16[640,768]{1,0:T(8,128)(2,1)}), bf16[2560,768]{1,0:T(8,128)(2,1)}) %all-gather.11.cloned.1.call-update) | async-done | bytes 3932176 | tf_op jit(solution)/shard_map/all_gather | solution.py:231
  499.5 6.2 multiply_reduce_fusion.6
  505.7 11.2 %all-reduce.2 = (f32[2560]{0:T(1024)S(1)}, f32[2560]{0:T(1024)S(1)}, f32[768]{0:T(1024)}) all-reduce(f32[2560]{0:T(1024)S(1)} %get-tuple-element.437, f32[2560]{0:T(1024)S(1)} %get-tuple-element.443, f32[768]{0:T(1024)S(1)} %get-tuple-element.438), channel_id=1, replica_groups=mesh['dp'=8,'tensor'=4] {'tensor'}, use_global_device_ids=true, to_apply=%region_30.31 | all-reduce | flops 5888 | bytes 47104 | tf_op jit(solution)/shard_map/psum | solution.py:236
  519.6 234.3 %while.38 = (s32[]{:T(128)}, f32[2560,3,64]{0,2,1:T(8,128)}, f32[2560,3,64]{0,2,1:T(8,128)}, bf16[5,512,3,64]{1,3,2,0:T(8,128)(2,1)}, s32[5]{0:T(128)S(1)}, /*in...) while((s32[]{:T(128)}, f32[2560,3,64]{0,2,1:T(8,128)}, ...), condition=%wide.region_33.34_spmd.clone.clone, body=%wide.region_31.33_spmd.clone.sunk.clone | while | flops 2558461440 | bytes 171972976 | solution.py:137
  523.9 8.9 fusion.138
  532.8 9.1 multiply_reduce_fusion.15
  542.0 9.6 multiply_convert_fusion.11
  554.4 6.5 fusion.141
  568.9 9.0 fusion.138
  577.9 9.1 multiply_reduce_fusion.15
  587.0 9.6 multiply_convert_fusion.11
  600.9 6.5 fusion.141
  616.2 9.0 fusion.138
  625.2 9.1 multiply_reduce_fusion.15
  634.3 9.6 multiply_convert_fusion.11
  648.2 6.5 fusion.141
  663.5 9.0 fusion.138
  672.5 9.1 multiply_reduce_fusion.15
  681.6 9.6 multiply_convert_fusion.11
  695.5 6.5 fusion.141
  710.9 9.0 fusion.138
  719.8 9.1 multiply_reduce_fusion.15
  728.9 9.6 multiply_convert_fusion.11
  742.9 6.5 fusion.141
  769.0 8.1 fusion.59
  777.1 9.7 fusion.53
  793.4 22.6 %all-reduce = (f32[192]{0:T(256)}, f32[768]{0:T(1024)}, f32[768]{0:T(1024)}) all-reduce(f32[192]{0:T(256)S(1)} %copy-done.37, f32[768]{0:T(1024)S(1)} %copy-done.36, f32[768]{0:T(1024)S(1)} %copy-done.35), channel_id=1, replica_groups=mesh['dp'=8,'tensor'=4] {'dp'}, use_global_device_ids=true, to_apply=%region_41.42 | all-reduce | flops 1728 | bytes 13824 | tf_op jit(solution)/shard_map/psum | solution.py:259
  818.3 40.4 %psum.127 = f32[768]{0:T(1024)} all-reduce(f32[768]{0:T(1024)S(1)} %get-tuple-element.440), channel_id=1, replica_groups=mesh['dp'=8,'tensor'=4] {'dp','tensor'}, use_global_device_ids=true, to_apply=%region_38.39 | all-reduce | flops 768 | bytes 6144 | tf_op jit(solution)/shard_map/psum | solution.py:262
  862.5 193.0 %all-reduce.8.cloned.1.call-done = (f32[768,576]{0,1:T(8,128)}, f32[192,768]{1,0:T(8,128)}, f32[768,768]{1,0:T(8,128)}, f32[768,768]{1,0:T(8,128)}) async-done(((f32[768,576]{0,1:T(8,128)}, f32[192,768]{1,0:T(8,128)}, f32[768,768]{1,0:T(8,128)}, f32[768,768]{1,0:T(8,128)}), (f32[768,576]{0,1:T(8,128)}, f32[192,768]{1,0:T(8,128)}, f32[768,768]{1,0:T(8,128)}, ...) | async-done | bytes 7077904 | tf_op jit(solution)/shard_map/psum | solution.py:259
  (263 shorter events, 188.6 us)
Async XLA Ops:
  7.2 299.3 %copy-start = (bf16[768,768]{1,0:T(8,128)(2,1)S(1)}, bf16[768,768]{1,0:T(8,128)(2,1)}, u32[]{:S(2)}) copy-start(bf16[768,768]{1,0:T(8,128)(2,1)} %param.24) | copy-start | bytes 3538948
  7.2 4.4 copy-start.43
  7.2 40.2 %copy-start.41 = (bf16[768,576]{0,1:T(8,128)(2,1)S(1)}, bf16[768,576]{0,1:T(8,128)(2,1)}, u32[]{:S(2)}) copy-start(bf16[768,576]{0,1:T(8,128)(2,1)} %param.18) | copy-start | bytes 2654212
  7.2 40.2 %all-gather.5.cloned.1.call-start = ((), (), s32[]{:S(2)}) async-start(), calls=%async_computation.4 | async-start | bytes 4915200 | tf_op jit(solution)/shard_map/all_gather | solution.py:169
  9.0 43.0 %copy-start.21 = (f32[640]{0:T(1024)}, f32[640]{0:T(1024)S(1)}, u32[]{:S(2)}) copy-start(f32[640]{0:T(1024)S(1)} %get-tuple-element.522) | copy-start | bytes 7684
  9.0 43.0 %copy-start.23 = (f32[640]{0:T(1024)}, f32[640]{0:T(1024)S(1)}, u32[]{:S(2)}) copy-start(f32[640]{0:T(1024)S(1)} %get-tuple-element.523) | copy-start | bytes 7684
  11.6 222.0 %reduce-scatter.5.cloned.1.call-start = ((), (), s32[]{:S(2)}) async-start(), calls=%async_computation.5 | async-start | bytes 9830400 | tf_op jit(solution)/shard_map/reduce_scatter | solution.py:183
  137.3 20.0 %copy-start.31 = (f32[192]{0:T(256)S(1)}, f32[192]{0:T(256)}, u32[]{:S(2)}) copy-start(f32[192]{0:T(256)} %param.19) | copy-start | bytes 2308
  157.3 359.7 %copy-start.17 = (f32[2560]{0:T(1024)}, f32[2560]{0:T(1024)S(1)}, u32[]{:S(2)}) copy-start(f32[2560]{0:T(1024)S(1)} %get-tuple-element.518) | copy-start | bytes 30724
  157.3 359.7 %copy-start.19 = (f32[2560]{0:T(1024)}, f32[2560]{0:T(1024)S(1)}, u32[]{:S(2)}) copy-start(f32[2560]{0:T(1024)S(1)} %get-tuple-element.519) | copy-start | bytes 30724
  163.3 73.7 %copy-start.30 = (f32[768]{0:T(1024)S(1)}, f32[768]{0:T(1024)}, u32[]{:S(2)}) copy-start(f32[768]{0:T(1024)} %param.21) | copy-start | bytes 9220
  163.3 108.1 %all-gather.7.cloned.1.call-start = ((), (), s32[]{:S(2)}) async-start(), calls=%async_computation.6 | async-start | bytes 4915200 | tf_op jit(solution)/shard_map/all_gather | solution.py:191
  238.3 68.2 %all-gather.9.cloned.1.call-start = ((), (), s32[]{:S(2)}) async-start(), calls=%async_computation.8 | async-start | bytes 4915200 | tf_op jit(solution)/shard_map/all_gather | solution.py:170
  238.9 67.6 %copy-start.33 = (f32[768]{0:T(1024)S(1)}, f32[768]{0:T(1024)}, u32[]{:S(2)}) copy-start(f32[768]{0:T(1024)} %param.23) | copy-start | bytes 9220
  238.9 178.0 %reduce-scatter.9.cloned.1.call-start = ((), (), s32[]{:S(2)}) async-start(), calls=%async_computation.9 | async-start | bytes 9830400 | tf_op jit(solution)/shard_map/reduce_scatter | solution.py:226
  292.5 54.2 %copy-start.25 = (f32[2560]{0:T(1024)}, f32[2560]{0:T(1024)S(1)}, u32[]{:S(2)}) copy-start(f32[2560]{0:T(1024)S(1)} %get-tuple-element.516) | copy-start | bytes 30724
  292.5 54.2 %copy-start.27 = (f32[2560]{0:T(1024)}, f32[2560]{0:T(1024)S(1)}, u32[]{:S(2)}) copy-start(f32[2560]{0:T(1024)S(1)} %get-tuple-element.517) | copy-start | bytes 30724
  329.0 12.2 %copy-start.40 = (bf16[768,768]{1,0:T(8,128)(2,1)S(1)}, bf16[768,768]{1,0:T(8,128)(2,1)}, u32[]{:S(2)}) copy-start(bf16[768,768]{1,0:T(8,128)(2,1)} %param.22) | copy-start | bytes 3538948
  346.7 115.5 %reduce-scatter.7.cloned.1.call-start = ((), (), s32[]{:S(2)}) async-start(), calls=%async_computation.7 | async-start | bytes 4915200 | tf_op jit(solution)/shard_map/reduce_scatter | solution.py:203
  355.5 106.7 %copy-start.11 = (bf16[640,768]{1,0:T(8,128)(2,1)S(1)}, bf16[640,768]{1,0:T(8,128)(2,1)}, u32[]{:S(2)}) copy-start(bf16[640,768]{1,0:T(8,128)(2,1)} %param.25) | copy-start | bytes 2949124
  355.5 144.0 %all-gather.11.cloned.1.call-start = ((), (), s32[]{:S(2)}) async-start(), calls=%async_computation.10 | async-start | bytes 4915200 | tf_op jit(solution)/shard_map/all_gather | solution.py:231
  466.3 349.7 %reduce-scatter.11.cloned.1.call-start = ((), (), s32[]{:S(2)}) async-start(), calls=%async_computation.11 | async-start | bytes 4915200 | tf_op jit(solution)/shard_map/reduce_scatter | solution.py:250
  554.3 6.5 copy-start.2
  600.9 6.5 copy-start.2
  607.5 4.6 copy-start.6
  648.2 6.5 copy-start.2
  654.8 4.6 copy-start.6
  695.5 6.5 copy-start.2
  702.1 4.6 copy-start.6
  742.9 6.5 copy-start.2
  749.4 4.6 copy-start.6
  754.0 6.1 copy-start.3
  768.9 8.2 copy-start.26
  768.9 8.2 copy-start.28
  768.9 8.2 copy-start.34
  768.9 286.6 %all-reduce.8.cloned.1.call-start = ((), (), s32[]{:S(2)}) async-start(), calls=%async_computation.12 | async-start | bytes 14155776 | tf_op jit(solution)/shard_map/psum | solution.py:259
  768.9 8.1 copy-start.39
  777.1 9.8 copy-start.4
  777.1 9.8 copy-start.10
  777.1 9.8 copy-start.18
  777.1 9.8 copy-start.20
  777.1 9.8 copy-start.32
  777.1 11.6 %copy-start.38 = (bf16[2560,768]{1,0:T(8,128)(2,1)S(1)}, bf16[2560,768]{1,0:T(8,128)(2,1)}, u32[]{:S(2)}) copy-start(bf16[2560,768]{1,0:T(8,128)(2,1)} %all-gather.5.cloned.1.call-done) | copy-start | bytes 11796484
  792.7 23.3 %copy-start.8 = (bf16[640,768]{1,0:T(8,128)(2,1)S(1)}, bf16[640,768]{1,0:T(8,128)(2,1)}, u32[]{:S(2)}) copy-start(bf16[640,768]{1,0:T(8,128)(2,1)} %param.15) | copy-start | bytes 2949124
  792.7 23.3 %copy-start.22 = (f32[640]{0:T(1024)S(1)}, f32[640]{0:T(1024)}, u32[]{:S(2)}) copy-start(f32[640]{0:T(1024)} %copy-done.21) | copy-start | bytes 7684
  792.8 23.3 %copy-start.24 = (f32[640]{0:T(1024)S(1)}, f32[640]{0:T(1024)}, u32[]{:S(2)}) copy-start(f32[640]{0:T(1024)} %copy-done.23) | copy-start | bytes 7684
  792.8 23.3 %copy-start.29 = (f32[768]{0:T(1024)S(1)}, f32[768]{0:T(1024)}, u32[]{:S(2)}) copy-start(f32[768]{0:T(1024)} %param.17) | copy-start | bytes 9220
  1055.5 5.2 copy-start.14
  (17 other events, 40.5 us)
Sparse Core Ops, SparseCore 0:
  11.7 35.6 all-gather.4
  163.4 70.0 reduce-scatter.4
  238.4 32.9 all-gather.6
  272.9 33.5 all-gather.8
  346.8 70.0 reduce-scatter.8
  419.3 42.8 reduce-scatter.6
  466.4 33.0 all-gather.10
  769.0 43.9 reduce-scatter.10
  818.5 236.8 all-reduce.7
where the time goes:
time: 1080 us; the launch traced here: 1070 us
  waiting for transfers between devices  481 us (45%)
  matrix products  294 us (27%)
  other arithmetic  120 us (11%)
  blocking collectives  107 us (10%)
  local copies, waits for them, and re-layouts  36.4 us (3%)
  loops' own time  15 us (1%)
  between operations  14.9 us (1%)
    psum x1, waiting for transfers between devices, local(): lax.psum((grad_qkv_part, grad_out_part, grad_attn_gain_part, grad_ffn_gai...  193 us
    reduce_scatter x1, waiting for transfers between devices, local(): lax.psum_scatter(jnp.dot(att_low, out_weight, preferred_element_type=jnp....  70.2 us
    dot_general x10, matrix products, block_scores(): jnp.einsum('qhe,khe->hqk', query_block, keys, preferred_element_type=jnp....  66.8 us
    reduce_scatter x1, waiting for transfers between devices, local(): lax.psum_scatter(contract_cols(grad_pre, up_weight), 'tensor', scatter_di...  61.3 us
    convert_element_type x5, other arithmetic, one_block(): grad_score = (weights * (grad_weights - jnp.sum(weights * grad_weights, a...  47.9 us
    dot_general x5, matrix products, one_block(): jnp.einsum('qhe,khe->hqk', grad_block, values, preferred_element_type=jnp...  44.8 us
    reduce_scatter x1, waiting for transfers between devices, local(): lax.psum_scatter(jnp.dot(lax.slice_in_dim(act_low, 0, lax.axis_size('tens...  42.4 us
    psum x1, blocking collectives, local(): grad_in_gain = lax.psum(grad_in_gain_part, ('dp', 'tensor'))  40.4 us
  transfers between devices with their start and end apart: 9, of which 8 were waited for; matrix products, arithmetic and copies ran while one was open for 5% of the time, Pallas kernels for 0%

commit v1 on v0

--- a/solution.py
+++ b/solution.py
@@ -3,14 +3,14 @@
 import jax
 import jax.numpy as jnp
 from jax import lax
+from jax.experimental import pallas as pl
+from jax.experimental.pallas import tpu as pltpu
 from jax.sharding import PartitionSpec as P
 
 D = 768
 HEAD_DIM = 64
 FF = 3072
 UNIT = 64
-MAXLEN = 2048
-QB = 512
 
 
 EPS = 1e-05
@@ -46,100 +46,219 @@
     )
 
 
-def segment_ids(counts, row_count):
-    ends = jnp.cumsum(counts * UNIT)
-    positions = jnp.arange(row_count, dtype=jnp.int32)
-    return jnp.sum((positions[:, None] >= ends[None, :]).astype(jnp.int32), axis=1)
-
-
-def split_heads(packed):
-    row_count = packed.shape[0]
-    head_count = packed.shape[1] // (3 * HEAD_DIM)
-    heads_view = packed.reshape(row_count, head_count, 3, HEAD_DIM)
-    return (heads_view[:, :, 0], heads_view[:, :, 1], heads_view[:, :, 2])
-
-
-def block_scores(queries, keys, segment, block_index):
-    row_count = queries.shape[0]
-    width = MAXLEN + QB
-    first_row = block_index * QB
-    key_start = jnp.clip(first_row + QB - width, 0, row_count - width)
-    query_block = lax.dynamic_slice_in_dim(queries, first_row, QB, 0)
-    query_segment = lax.dynamic_slice_in_dim(segment, first_row, QB, 0)
-    query_pos = first_row + jnp.arange(QB, dtype=jnp.int32)
-    key_pos = key_start + jnp.arange(width, dtype=jnp.int32)
-    allowed = (query_segment[:, None] == segment[None, :]) & (
-        key_pos[None, :] <= query_pos[:, None]
-    )
-    score = jnp.einsum("qhe,khe->hqk", query_block, keys, preferred_element_type=jnp.float32) * (
-        1.0 / float(HEAD_DIM) ** 0.5
-    )
-    return (jnp.where(allowed[None], score, -1000000000.0), query_block, keys, key_start)
-
-
-def attention_forward(packed, segment):
-    queries, keys, values = split_heads(packed)
-
-    def one_block(block_index):
-        score, query_block, key_window, key_start = block_scores(
-            queries, keys, segment, block_index
-        )
-        top_score = jnp.max(score, axis=2, keepdims=True)
-        exponent = jnp.exp(score - top_score)
-        row_total = jnp.sum(exponent, axis=2, keepdims=True)
-        weights = (exponent / row_total).astype(jnp.bfloat16)
-        mixed = jnp.einsum("hqk,khe->qhe", weights, values, preferred_element_type=jnp.float32)
-        return (mixed, (top_score + jnp.log(row_total))[:, :, 0])
-
-    mixed, log_total = lax.map(one_block, jnp.arange(packed.shape[0] // QB, dtype=jnp.int32))
-    return (mixed.reshape(packed.shape[0], -1), log_total)
-
-
-def attention_backward(packed, segment, log_total, grad_mixed):
-    queries, keys, values = split_heads(packed)
-    row_count = packed.shape[0]
-    head_count = queries.shape[1]
-    grad_heads = grad_mixed.reshape(row_count, head_count, HEAD_DIM)
-    scale = 1.0 / float(HEAD_DIM) ** 0.5
-
-    def one_block(carry, block_index):
-        grad_keys, grad_values = carry
-        score, query_block, key_window, key_start = block_scores(
-            queries, keys, segment, block_index
-        )
-        grad_block = lax.dynamic_slice_in_dim(grad_heads, block_index * QB, QB, 0)
-        weights = jnp.exp(score - log_total[block_index][:, :, None])
-        grad_weights = jnp.einsum(
-            "qhe,khe->hqk", grad_block, values, preferred_element_type=jnp.float32
-        )
-        grad_score = (
-            weights * (grad_weights - jnp.sum(weights * grad_weights, axis=2, keepdims=True))
-        ).astype(jnp.bfloat16)
-        grad_query = (
-            jnp.einsum("hqk,khe->qhe", grad_score, key_window, preferred_element_type=jnp.float32)
-            * scale
-        )
-        grad_key = (
-            jnp.einsum("hqk,qhe->khe", grad_score, query_block, preferred_element_type=jnp.float32)
-            * scale
-        )
-        grad_value = jnp.einsum(
-            "hqk,qhe->khe",
-            weights.astype(jnp.bfloat16),
-            grad_block,
-            preferred_element_type=jnp.float32,
-        )
-        grad_keys = grad_keys + grad_key
-        grad_values = grad_values + grad_value
-        return ((grad_keys, grad_values), grad_query)
-
-    zeros = jnp.zeros((row_count, head_count, HEAD_DIM), jnp.float32)
-    (grad_keys, grad_values), grad_queries = lax.scan(
-        one_block, (zeros, zeros), jnp.arange(row_count // QB, dtype=jnp.int32)
-    )
-    grad_queries = grad_queries.reshape(row_count, head_count, HEAD_DIM)
-    stacked = jnp.stack((grad_queries, grad_keys, grad_values), axis=2)
-    return stacked.reshape(row_count, 3 * head_count * HEAD_DIM).astype(jnp.bfloat16)
+NEG = -1e30
+def seq_bounds(len_ref):
+    ends, total = [], 0
+    for s in range(len_ref.shape[1]):
+        total = total + len_ref[0, s] * UNIT
+        ends.append(total)
+    return ends
+
+
+def start_of(ends, row):
+    at = 0
+    for end in ends:
+        at = jnp.where(row >= end, end, at)
+    return at
+
+
+def end_of(ends, row):
+    at = ends[-1]
+    for end in reversed(ends):
+        at = jnp.where(row < end, end, at)
+    return at
+
+
+def dot(a, b):
+    return lax.dot_general(a, b, (((1,), (0,)), ((), ())), preferred_element_type=jnp.float32)
+
+
+def fwd_kernel(bq, bk, len_ref, qkv_ref, o_ref, lse_ref, k_s, qt_s, vt_s, acc_s, m_s):
+    rows = qkv_ref.shape[0]
+    heads = k_s.shape[0]
+    ends = seq_bounds(len_ref)
+    ones = (lax.broadcasted_iota(jnp.int32, (16, bq), 0) == 0).astype(jnp.float32).astype(jnp.bfloat16)
+
+    def stage(i, _):
+        at = pl.ds(pl.multiple_of(i * bq, bq), bq)
+        x = qkv_ref[at, :]
+        for h in range(heads):
+            base = h * 3 * HEAD_DIM
+            q = x[:, base : base + HEAD_DIM] * jnp.bfloat16(0.125)
+            qt_s[h, :, at] = q.T
+            k_s[h, at, :] = x[:, base + HEAD_DIM : base + 2 * HEAD_DIM]
+            vt_s[h, :HEAD_DIM, at] = x[:, base + 2 * HEAD_DIM : base + 3 * HEAD_DIM].T
+            vt_s[h, HEAD_DIM:, at] = ones
+        return 0
+
+    lax.fori_loop(0, rows // bq, stage, 0)
+
+    def query_block(i, _):
+        first = pl.multiple_of(i * bq, bq)
+        at = pl.ds(first, bq)
+        q_pos = first + lax.broadcasted_iota(jnp.int32, (1, bq), 1)
+        q_start = start_of(ends, q_pos)
+        lo = start_of(ends, first)
+        hi = start_of(ends, first + bq - 1)
+        for h in range(heads):
+            acc_s[h] = jnp.zeros_like(acc_s[h])
+            m_s[h] = jnp.full_like(m_s[h], NEG)
+
+        def step(masked, c, _):
+            c0 = pl.multiple_of(c * bk, bk)
+            for h in range(heads):
+                s = dot(k_s[h, pl.ds(c0, bk), :], qt_s[h, :, at])
+                if masked:
+                    k_pos = c0 + lax.broadcasted_iota(jnp.int32, (bk, 1), 0)
+                    s = jnp.where((k_pos <= q_pos) & (k_pos >= q_start), s, NEG)
+                old = m_s[h]
+                new = jnp.maximum(old, jnp.max(s, axis=0, keepdims=True))
+                p = jnp.exp(s - new).astype(jnp.bfloat16)
+                m_s[h] = new
+                acc_s[h] = acc_s[h] * jnp.exp(old - new) + dot(vt_s[h, :, pl.ds(c0, bk)], p)
+            return 0
+
+        c_lo = lo // bk
+        c_diag = first // bk
+        c_end = (first + bq - 1) // bk + 1
+        c_int = jnp.minimum((hi + bk - 1) // bk, c_diag)
+        lax.fori_loop(c_lo, c_int, partial(step, True), 0)
+        lax.fori_loop(c_int, c_diag, partial(step, False), 0)
+        lax.fori_loop(jnp.maximum(c_diag, c_lo), c_end, partial(step, True), 0)
+        outs = []
+        for h in range(heads):
+            acc = acc_s[h]
+            total = acc[HEAD_DIM : HEAD_DIM + 1, :]
+            outs.append((acc[:HEAD_DIM, :] / total).T)
+            lse_ref[h : h + 1, at] = m_s[h] + jnp.log(total)
+        o_ref[at, :] = jnp.concatenate(outs, axis=1).astype(o_ref.dtype)
+        return 0
+
+    lax.fori_loop(0, rows // bq, query_block, 0)
+
+
+def attn_fwd(packed, lengths, bq=256, bk=256, out_dtype=jnp.float32):
+    rows = packed.shape[0]
+    heads = packed.shape[1] // (3 * HEAD_DIM)
+    return pl.pallas_call(
+        partial(fwd_kernel, bq, bk),
+        out_shape=(
+            jax.ShapeDtypeStruct((rows, heads * HEAD_DIM), out_dtype),
+            jax.ShapeDtypeStruct((8, rows), jnp.float32),
+        ),
+        in_specs=[pl.BlockSpec(memory_space=pltpu.SMEM), pl.BlockSpec(memory_space=pltpu.VMEM)],
+        out_specs=[pl.BlockSpec(memory_space=pltpu.VMEM)] * 2,
+        scratch_shapes=[
+            pltpu.VMEM((heads, rows, HEAD_DIM), jnp.bfloat16),
+            pltpu.VMEM((heads, HEAD_DIM, rows), jnp.bfloat16),
+            pltpu.VMEM((heads, HEAD_DIM + 16, rows), jnp.bfloat16),
+            pltpu.VMEM((heads, HEAD_DIM + 16, bq), jnp.float32),
+            pltpu.VMEM((heads, 1, bq), jnp.float32),
+        ],
+        compiler_params=pltpu.CompilerParams(vmem_limit_bytes=48 << 20),
+        name="attn_fwd",
+    )(lengths, packed)
+
+
+def bwd_kernel(bq, bk, len_ref, qkv_ref, o_ref, lse_ref, do_ref, out_ref,
+               q_s, k_s, v_s, do_s, qt_s, kt_s, dot_s, d_s, dqt_s, dk_s, dv_s):
+    rows = qkv_ref.shape[0]
+    heads = k_s.shape[0]
+    ends = seq_bounds(len_ref)
+    scale = jnp.bfloat16(0.125)
+
+    def stage(i, _):
+        at = pl.ds(pl.multiple_of(i * bq, bq), bq)
+        x = qkv_ref[at, :]
+        g = do_ref[at, :]
+        prod = g.astype(jnp.float32) * o_ref[at, :].astype(jnp.float32)
+        for h in range(heads):
+            base = h * 3 * HEAD_DIM
+            q = x[:, base : base + HEAD_DIM] * scale
+            k = x[:, base + HEAD_DIM : base + 2 * HEAD_DIM]
+            d = g[:, h * HEAD_DIM : (h + 1) * HEAD_DIM]
+            q_s[h, at, :] = q
+            k_s[h, at, :] = k
+            v_s[h, at, :] = x[:, base + 2 * HEAD_DIM : base + 3 * HEAD_DIM]
+            do_s[h, at, :] = d
+            qt_s[h, :, at] = q.T
+            kt_s[h, :, at] = (k * scale).T
+            dot_s[h, :, at] = d.T
+            d_s[h, :, at] = jnp.sum(prod[:, h * HEAD_DIM : (h + 1) * HEAD_DIM].T, axis=0, keepdims=True)
+            dqt_s[h, :, at] = jnp.zeros((HEAD_DIM, bq), jnp.float32)
+        return 0
+
+    lax.fori_loop(0, rows // bq, stage, 0)
+
+    def key_block(j, _):
+        c0 = pl.multiple_of(j * bk, bk)
+        kat = pl.ds(c0, bk)
+        for h in range(heads):
+            dk_s[h, kat, :] = jnp.zeros((bk, HEAD_DIM), jnp.float32)
+            dv_s[h, kat, :] = jnp.zeros((bk, HEAD_DIM), jnp.float32)
+
+        def step(masked, i, _):
+            first = pl.multiple_of(i * bq, bq)
+            at = pl.ds(first, bq)
+            if masked:
+                q_pos = first + lax.broadcasted_iota(jnp.int32, (1, bq), 1)
+                q_start = start_of(ends, q_pos)
+                k_pos = c0 + lax.broadcasted_iota(jnp.int32, (bk, 1), 0)
+                keep = (k_pos <= q_pos) & (k_pos >= q_start)
+            for h in range(heads):
+                s = dot(k_s[h, kat, :], qt_s[h, :, at]) - lse_ref[h : h + 1, at]
+                if masked:
+                    s = jnp.where(keep, s, NEG)
+                p = jnp.exp(s)
+                dp = dot(v_s[h, kat, :], dot_s[h, :, at])
+                ds = (p * (dp - d_s[h, :, at])).astype(jnp.bfloat16)
+                dv_s[h, kat, :] += dot(p.astype(jnp.bfloat16), do_s[h, at, :])
+                dk_s[h, kat, :] += dot(ds, q_s[h, at, :])
+                dqt_s[h, :, at] += dot(kt_s[h, :, kat], ds)
+            return 0
+
+        i_diag = c0 // bq
+        i_after = (c0 + bk - 1) // bq + 1
+        i_end = (end_of(ends, c0 + bk - 1) + bq - 1) // bq
+        i_int = jnp.maximum(end_of(ends, c0) // bq, i_after)
+        i_int = jnp.minimum(i_int, i_end)
+        lax.fori_loop(i_diag, i_after, partial(step, True), 0)
+        lax.fori_loop(i_after, i_int, partial(step, False), 0)
+        lax.fori_loop(i_int, i_end, partial(step, True), 0)
+        return 0
+
+    lax.fori_loop(0, rows // bk, key_block, 0)
+
+    def finish(i, _):
+        at = pl.ds(pl.multiple_of(i * bq, bq), bq)
+        parts = []
+        for h in range(heads):
+            parts += [dqt_s[h, :, at].T, dk_s[h, at, :], dv_s[h, at, :]]
+        out_ref[at, :] = jnp.concatenate(parts, axis=1).astype(out_ref.dtype)
+        return 0
+
+    lax.fori_loop(0, rows // bq, finish, 0)
+
+
+def attn_bwd(packed, lengths, att, lse, d_att, bq=256, bk=256):
+    rows = packed.shape[0]
+    heads = packed.shape[1] // (3 * HEAD_DIM)
+    row_major = pltpu.VMEM((heads, rows, HEAD_DIM), jnp.bfloat16)
+    col_major = pltpu.VMEM((heads, HEAD_DIM, rows), jnp.bfloat16)
+    return pl.pallas_call(
+        partial(bwd_kernel, bq, bk),
+        out_shape=jax.ShapeDtypeStruct(packed.shape, jnp.bfloat16),
+        in_specs=[pl.BlockSpec(memory_space=pltpu.SMEM)] + [pl.BlockSpec(memory_space=pltpu.VMEM)] * 4,
+        out_specs=pl.BlockSpec(memory_space=pltpu.VMEM),
+        scratch_shapes=[row_major] * 4 + [col_major] * 3 + [
+            pltpu.VMEM((heads, 1, rows), jnp.float32),
+            pltpu.VMEM((heads, HEAD_DIM, rows), jnp.float32),
+            pltpu.VMEM((heads, rows, HEAD_DIM), jnp.float32),
+            pltpu.VMEM((heads, rows, HEAD_DIM), jnp.float32),
+        ],
+        compiler_params=pltpu.CompilerParams(vmem_limit_bytes=56 << 20),
+        name="attn_bwd",
+    )(lengths, packed, att, lse, d_att)
 
 
 def ffn_totals(grad_up, grad_down, grad_hidden):
@@ -162,7 +281,6 @@
     tensor_size = lax.axis_size("tensor")
     own_rows = tokens.shape[0]
     group_rows = own_rows * tensor_size
-    segment = segment_ids(lengths[0], group_rows)
     residual = tokens.astype(jnp.float32)
     in_unit, in_scale, in_normed = normalize(residual, in_gain)
     gathered_in, gathered_grad = (
@@ -172,7 +290,7 @@
     packed = jnp.dot(gathered_in, qkv_weight, preferred_element_type=jnp.float32).astype(
         jnp.bfloat16
     )
-    attended, log_total = attention_forward(packed, segment)
+    attended, log_total = attn_fwd(packed, lengths, 512, 512)
     att_sum, att_square = lax.psum(
         (jnp.sum(attended, axis=1), jnp.sum(attended * attended, axis=1)), "tensor"
     )
@@ -245,7 +363,7 @@
         att_scale[:, None]
         * (weighted_att - (first_att / D)[:, None] - att_unit * (second_att / D)[:, None])
     ).astype(jnp.bfloat16)
-    grad_packed = attention_backward(packed, segment, log_total, grad_attended)
+    grad_packed = attn_bwd(packed, lengths, attended, log_total, grad_attended, 512, 256)
     grad_qkv_part = contract_rows(gathered_in, grad_packed)
     grad_in_normed = lax.psum_scatter(
         contract_cols(grad_packed, qkv_weight).astype(jnp.bfloat16),

time: 1080 us -> 818 us (0.76)
  matrix products: 294 us -> 83.7 us
  other arithmetic: 120 us -> 36 us
  Pallas kernels: 0 us -> 71.2 us
  local copies, waits for them, and re-layouts: 36.4 us -> 11.4 us
  loops' own time: 15 us -> 0 us
    dot_general x35 -> x0, matrix products: 213 us -> none  [the longest x10 66.8 us: block_scores(): jnp.einsum('qhe,khe->hqk', query_block, keys, preferred_element_type=jnp....]
    pallas_call x0 -> x2, Pallas kernels: none -> 71.2 us  [the longest x1 41.3 us: attn_bwd(): pl.pallas_call(partial(bwd_kernel, bq, bk), out_shape=jax.ShapeDtypeStruc...]
    convert_element_type x5 -> x0, other arithmetic: 47.9 us -> none  [one_block(): grad_score = (weights * (grad_weights - jnp.sum(weights * grad_weights, a...]
    reduce_sum x6 -> x0, other arithmetic: 21.8 us -> none  [the longest x5 21.6 us: one_block(): row_total = jnp.sum(exponent, axis=2, keepdims=True)]
    another operation x2 -> x0, loops' own time: 15 us -> none  [the longest x1 11.5 us: attention_backward(): lax.scan(one_block, (zeros, zeros), jnp.arange(row_count // QB, dtype=jnp...]
    and x10 -> x0, other arithmetic: 11.5 us -> none  [block_scores(): (query_segment[:, None] == segment[None, :]) & (key_pos[None, :] <= query...]
  transfers between devices with their start and end apart: 9 -> 9, of which waited for: 8 -> 8; matrix products, arithmetic and copies ran while one was open for 5% -> 6% of each run, Pallas kernels for 0% -> 0%
where the time goes in v1:
time: 818 us; the launch traced here: 809 us
  waiting for transfers between devices  482 us (59%)
  blocking collectives  108 us (13%)
  matrix products  83.7 us (10%)
  Pallas kernels  71.2 us (9%)
  other arithmetic  36 us (4%)
  between operations  14.6 us (2%)
  local copies, waits for them, and re-layouts  11.4 us (1%)
    psum x1, waiting for transfers between devices, local(): lax.psum((grad_qkv_part, grad_out_part, grad_attn_gain_part, grad_ffn_gai...  194 us
    reduce_scatter x1, waiting for transfers between devices, local(): lax.psum_scatter(jnp.dot(att_low, out_weight, preferred_element_type=jnp....  69.2 us
    reduce_scatter x1, waiting for transfers between devices, local(): lax.psum_scatter(contract_cols(grad_pre, up_weight), 'tensor', scatter_di...  61.1 us
    reduce_scatter x1, waiting for transfers between devices, local(): lax.psum_scatter(jnp.dot(lax.slice_in_dim(act_low, 0, lax.axis_size('tens...  42.9 us
    pallas_call x1, Pallas kernels, attn_bwd(): pl.pallas_call(partial(bwd_kernel, bq, bk), out_shape=jax.ShapeDtypeStruc...  41.3 us
    psum x1, blocking collectives, local(): grad_in_gain = lax.psum(grad_in_gain_part, ('dp', 'tensor'))  39.9 us
    all_gather x1, waiting for transfers between devices, local(): lax.all_gather(in_normed.astype(jnp.bfloat16), 'tensor', axis=0, tiled=True)  35.8 us
    all_gather x1, waiting for transfers between devices, local(): lax.all_gather(grad_middle.astype(jnp.bfloat16), 'tensor', axis=0, tiled=...  33.1 us
  transfers between devices with their start and end apart: 9, of which 8 were waited for; matrix products, arithmetic and copies ran while one was open for 6% of the time, Pallas kernels for 0%

profile of v1, /device:TPU:0, one launch (start us, length us, event | category | flops | bytes accessed | tf_op | source)
XLA Modules:
  0.0 808.7 jit_solution(9117596900448095550)
XLA Ops:
  7.3 1.7 convert_reduce_fusion
  9.0 2.5 fusion.18
  11.6 35.8 %all-gather.5.cloned.1.call-done = bf16[2560,768]{1,0:T(8,128)(2,1)} async-done(((bf16[640,768]{1,0:T(8,128)(2,1)}), bf16[2560,768]{1,0:T(8,128)(2,1)}) %all-gather.5.cloned.1.call-update) | async-done | bytes 3932176 | tf_op jit(solution)/shard_map/all_gather | solution.py:287
  47.4 5.4 convolution_convert_fusion.2.qkv_ref
  52.8 29.9 %attn_fwd.1 = (f32[2560,192]{1,0:T(8,128)S(1)}, f32[8,2560]{1,0:T(8,128)S(1)}) custom-call(s32[1,5]{1,0:T(1,128)S(1)} %copy-done.6, bf16[2560,576]{1,0:T(8,128)(2,1)S(1)} %convolution_convert_fusion.2.qkv_ref), custom_call_target="tpu_custom_call" | custom-call | tf_op jit(solution)/shard_map/attn_fwd/pallas_call | solution.py:143
  82.7 1.4 copy-done.2
  84.1 0.7 fusion.24
  84.9 10.3 %all-reduce.5 = (f32[2560]{0:T(1024)S(1)}, f32[2560]{0:T(1024)S(1)}) all-reduce(f32[2560]{0:T(1024)S(1)} %get-tuple-element.25, f32[2560]{0:T(1024)S(1)} %get-tuple-element.24), channel_id=1, replica_groups=mesh['dp'=8,'tensor'=4] {'tensor'}, use_global_device_ids=true, to_apply=%region_5.0 | all-reduce | flops 5120 | bytes 40960 | tf_op jit(solution)/shard_map/psum | solution.py:294
  95.3 6.4 fusion.21
  101.7 69.2 %reduce-scatter.5.cloned.1.call-done = f32[640,768]{1,0:T(8,128)} async-done(((f32[2560,768]{1,0:T(8,128)}), f32[640,768]{1,0:T(8,128)}) %reduce-scatter.5.cloned.1.call-update) | async-done | bytes 1966096 | tf_op jit(solution)/shard_map/reduce_scatter | solution.py:301
  170.9 2.2 fusion.25
  173.2 1.3 multiply_convert_fusion.3
  175.5 32.1 %all-gather.7.cloned.1.call-done = bf16[2560,768]{1,0:T(8,128)(2,1)} async-done(((bf16[640,768]{1,0:T(8,128)(2,1)}), bf16[2560,768]{1,0:T(8,128)(2,1)}) %all-gather.7.cloned.1.call-update) | async-done | bytes 3932176 | tf_op jit(solution)/shard_map/all_gather | solution.py:309
  207.6 9.4 %fusion.23 = (f32[2560]{0:T(1024)S(1)}, f32[2560]{0:T(1024)S(1)}, f32[2560,768]{0,1:T(8,128)}) fusion(bf16[2560,768]{1,0:T(8,128)(2,1)} %all-gather.7.cloned.1.call-done, bf16[768,768]{1,0:T(8,128)(2,1)} %param.18), kind=kOutput, calls=%fused_computation.72 | convolution fusion | flops 3041520640 | bytes 12996608 | tf_op jit(solution)/shard_map/dot_general | solution.py:310
  217.1 11.6 %all-reduce.4 = (f32[2560]{0:T(1024)S(1)}, f32[2560]{0:T(1024)S(1)}) all-reduce(f32[2560]{0:T(1024)S(1)} %get-tuple-element.18, f32[2560]{0:T(1024)S(1)} %get-tuple-element.17), channel_id=1, replica_groups=mesh['dp'=8,'tensor'=4] {'tensor'}, use_global_device_ids=true, to_apply=%region_12.0 | all-reduce | flops 5120 | bytes 40960 | tf_op jit(solution)/shard_map/psum | solution.py:312
  228.7 14.0 %all-gather.9.cloned.1.call-done = bf16[2560,768]{1,0:T(8,128)(2,1)} async-done(((bf16[640,768]{1,0:T(8,128)(2,1)}), bf16[2560,768]{1,0:T(8,128)(2,1)}) %all-gather.9.cloned.1.call-update) | async-done | bytes 3932176 | tf_op jit(solution)/shard_map/all_gather | solution.py:288
  242.7 11.6 %multiply_reduce_fusion = (f32[768]{0:T(1024)}, f32[2560]{0:T(1024)S(1)}, f32[2560]{0:T(1024)S(1)}, f32[2560,768]{0,1:T(8,128)}) fusion(f32[2560]{0:T(1024)S(1)} %get-tuple-element.55, f32[2560]{0:T(1024)S(1)} %get-tuple-element.54, f32[2560,768]{0,1:T(8,128)} %get-tuple-element.62, f32[768]{0:T(1024)S(1)} %copy-done.19, ...), kind=kOutput, calls=%fused_computation.9 | convolution fusion | flops 3051350272 | bytes 20887552 | tf_op jit(solution)/shard_map/dot_general | solution.py:26
  254.3 10.9 %all-reduce.3 = (f32[2560]{0:T(1024)S(1)}, f32[2560]{0:T(1024)}) all-reduce(f32[2560]{0:T(1024)S(1)} %get-tuple-element.15, f32[2560]{0:T(1024)S(1)} %get-tuple-element.16), channel_id=1, replica_groups=mesh['dp'=8,'tensor'=4] {'tensor'}, use_global_device_ids=true, to_apply=%region_17.0 | all-reduce | flops 5120 | bytes 40960 | tf_op jit(solution)/shard_map/psum | solution.py:336
  265.2 0.7 broadcast_multiply_fusion
  266.0 10.2 %fusion.6 = bf16[2560,768]{0,1:T(8,128)(2,1)S(1)} fusion(f32[2560,768]{0,1:T(8,128)} %get-tuple-element.62, f32[2560,768]{0,1:T(8,128)} %get-tuple-element.63, f32[2560]{0:T(1024)S(1)} %get-tuple-element.65, f32[2560]{0:T(1024)S(1)} %get-tuple-element.66, f32[768]{0:T(1024)S(1)} %copy-done.19, f32[2560]{0:T(1024)S(1)} %get-tuple-element.55, ...), kind=kLoop, calls=%fused_computation.8 | loop fusion | flops 55050240 | bytes 19704832 | tf_op jit(solution)/shard_map/convert_element_type | solution.py:342
  276.2 2.0 copy-done.9
  278.1 5.5 fusion.27
  283.9 8.7 %convolution_convert_fusion = bf16[2560,768]{1,0:T(8,128)(2,1)} fusion(bf16[768,768]{1,0:T(8,128)(2,1)S(1)} %copy-done, f32[768]{0:T(1024)S(1)} %copy-done.19, f32[2560]{0:T(1024)S(1)} %get-tuple-element.55, f32[2560]{0:T(1024)S(1)} %get-tuple-element.54, f32[2560,768]{0,1:T(8,128)} %get-tuple-element.62), kind=kOutput, calls=%fused_computation.16 | convolution fusion | flops 3045457920 | bytes 12999680 | tf_op jit(solution)/shard_map/dot_general | solution.py:322
  292.7 61.1 %reduce-scatter.9.cloned.1.call-done = f32[640,768]{1,0:T(8,128)} async-done(((f32[2560,768]{1,0:T(8,128)}), f32[640,768]{1,0:T(8,128)}) %reduce-scatter.9.cloned.1.call-update) | async-done | bytes 1966096 | tf_op jit(solution)/shard_map/reduce_scatter | solution.py:344
  353.8 2.3 multiply_reduce_fusion.8
  356.2 42.9 %reduce-scatter.7.cloned.1.call-done = bf16[640,768]{1,0:T(8,128)(2,1)} async-done(((bf16[2560,768]{1,0:T(8,128)(2,1)}), bf16[640,768]{1,0:T(8,128)(2,1)}) %reduce-scatter.7.cloned.1.call-update) | async-done | bytes 983056 | tf_op jit(solution)/shard_map/reduce_scatter | solution.py:321
  399.1 3.7 fusion.26
  402.9 33.1 %all-gather.11.cloned.1.call-done = bf16[2560,768]{1,0:T(8,128)(2,1)} async-done(((bf16[640,768]{1,0:T(8,128)(2,1)}), bf16[2560,768]{1,0:T(8,128)(2,1)}) %all-gather.11.cloned.1.call-update) | async-done | bytes 3932176 | tf_op jit(solution)/shard_map/all_gather | solution.py:349
  436.0 6.0 multiply_reduce_fusion.4
  442.0 10.7 %all-reduce.2 = (f32[2560]{0:T(1024)S(1)}, f32[2560]{0:T(1024)S(1)}, f32[768]{0:T(1024)S(1)}) all-reduce(f32[2560]{0:T(1024)S(1)} %get-tuple-element.20, f32[2560]{0:T(1024)S(1)} %get-tuple-element.23, f32[768]{0:T(1024)S(1)} %get-tuple-element.21), channel_id=1, replica_groups=mesh['dp'=8,'tensor'=4] {'tensor'}, use_global_device_ids=true, to_apply=%region_24.0 | all-reduce | flops 5888 | bytes 47104 | tf_op jit(solution)/shard_map/psum | solution.py:354
  452.7 5.1 multiply_convert_fusion.1.do_ref
  457.8 41.3 %attn_bwd.1 = bf16[2560,576]{1,0:T(8,128)(2,1)} custom-call(s32[1,5]{1,0:T(1,128)} %len_ref.3, bf16[2560,576]{1,0:T(8,128)(2,1)} %copy-done.4, f32[2560,192]{1,0:T(8,128)} %copy-done.2, f32[8,2560]{1,0:T(8,128)} %copy-done.5, bf16[2560,192]{1,0:T(8,128)(2,1)} %multiply_convert_fusion.1.do_ref), custom_call_target="tpu_custom_call" | custom-call | tf_op jit(solution)/shard_map/attn_bwd/pallas_call | solution.py:248
  499.2 7.1 convolution_convert_fusion.1
  506.7 8.1 %fusion.29 = f32[768,768]{1,0:T(8,128)} fusion(bf16[2560,768]{1,0:T(8,128)(2,1)} %all-gather.7.cloned.1.call-done, bf16[2560,768]{0,1:T(8,128)(2,1)} %copy-done.9), kind=kOutput, calls=%fused_computation.78 | convolution fusion | flops 3019898880 | bytes 10223616 | tf_op jit(solution)/shard_map/dot_general | solution.py:20
  514.8 9.1 %fusion.22 = f32[768,768]{1,0:T(8,128)} fusion(bf16[2560,768]{1,0:T(8,128)(2,1)S(1)} %copy-done.22, f32[768]{0:T(1024)S(1)} %copy-done.19, f32[2560]{0:T(1024)S(1)} %get-tuple-element.55, f32[2560]{0:T(1024)S(1)} %get-tuple-element.54, f32[2560,768]{0,1:T(8,128)} %get-tuple-element.62), kind=kOutput, calls=%fused_computation.71 | convolution fusion | flops 3043491840 | bytes 14179328 | tf_op jit(solution)/shard_map/dot_general | solution.py:20
  523.9 2.7 fusion.20
  526.5 0.7 copy-done.21
  527.2 3.7 fusion.28
  530.9 0.7 copy-done.20
  531.6 24.6 %all-reduce = (f32[192]{0:T(256)}, f32[768]{0:T(1024)}, f32[768]{0:T(1024)}) all-reduce(f32[192]{0:T(256)S(1)} %get-tuple-element.19, f32[768]{0:T(1024)S(1)} %get-tuple-element.43, f32[768]{0:T(1024)S(1)} %copy-done.20), channel_id=1, replica_groups=mesh['dp'=8,'tensor'=4] {'dp'}, use_global_device_ids=true, to_apply=%region_32.0 | all-reduce | flops 1728 | bytes 13824 | tf_op jit(solution)/shard_map/psum | solution.py:377
  556.2 2.2 fusion.14
  558.4 39.9 %psum.127 = f32[768]{0:T(1024)} all-reduce(f32[768]{0:T(1024)S(1)} %get-tuple-element.26), channel_id=1, replica_groups=mesh['dp'=8,'tensor'=4] {'dp','tensor'}, use_global_device_ids=true, to_apply=%region_29.0 | all-reduce | flops 768 | bytes 6144 | tf_op jit(solution)/shard_map/psum | solution.py:380
  598.4 3.2 fusion.12
  601.6 193.5 %all-reduce.8.cloned.1.call-done = (f32[768,576]{0,1:T(8,128)}, f32[192,768]{1,0:T(8,128)}, f32[768,768]{1,0:T(8,128)}, f32[768,768]{1,0:T(8,128)}) async-done(((f32[768,576]{0,1:T(8,128)}, f32[192,768]{1,0:T(8,128)}, f32[768,768]{1,0:T(8,128)}, f32[768,768]{1,0:T(8,128)}), (f32[768,576]{0,1:T(8,128)}, f32[192,768]{1,0:T(8,128)}, f32[768,768]{1,0:T(8,128)}, ...) | async-done | bytes 7077904 | tf_op jit(solution)/shard_map/psum | solution.py:377
  795.1 2.9 copy.30
  798.1 0.8 copy.31
  798.9 1.4 copy.32
  800.3 1.4 copy.33
  (79 shorter events, 2.1 us)
Async XLA Ops:
  7.2 235.5 %copy-start = (bf16[768,768]{1,0:T(8,128)(2,1)S(1)}, bf16[768,768]{1,0:T(8,128)(2,1)}, u32[]{:S(2)}) copy-start(bf16[768,768]{1,0:T(8,128)(2,1)} %param.20) | copy-start | bytes 3538948
  7.2 40.2 %copy-start.25 = (bf16[768,576]{0,1:T(8,128)(2,1)S(1)}, bf16[768,576]{0,1:T(8,128)(2,1)}, u32[]{:S(2)}) copy-start(bf16[768,576]{0,1:T(8,128)(2,1)} %param.14) | copy-start | bytes 2654212
  7.2 40.2 %all-gather.5.cloned.1.call-start = ((), (), s32[]{:S(2)}) async-start(), calls=%async_computation.4 | async-start | bytes 4915200 | tf_op jit(solution)/shard_map/all_gather | solution.py:287
  11.5 41.2 %copy-start.6 = (s32[1,5]{1,0:T(1,128)S(1)}, s32[1,5]{1,0:T(1,128)}, u32[]{:S(2)}) copy-start(s32[1,5]{1,0:T(1,128)} %len_ref.3) | copy-start | bytes 64
  11.5 159.4 %reduce-scatter.5.cloned.1.call-start = ((), (), s32[]{:S(2)}) async-start(), calls=%async_computation.5 | async-start | bytes 9830400 | tf_op jit(solution)/shard_map/reduce_scatter | solution.py:301
  52.8 32.1 %copy-start.4 = (bf16[2560,576]{1,0:T(8,128)(2,1)}, bf16[2560,576]{1,0:T(8,128)(2,1)S(1)}, u32[]{:S(2)}) copy-start(bf16[2560,576]{1,0:T(8,128)(2,1)S(1)} %convolution_convert_fusion.2.qkv_ref) | copy-start | bytes 8847364
  52.8 42.5 %copy-start.15 = (bf16[192,768]{1,0:T(8,128)(2,1)S(1)}, bf16[192,768]{1,0:T(8,128)(2,1)}, u32[]{:S(2)}) copy-start(bf16[192,768]{1,0:T(8,128)(2,1)} %param.16) | copy-start | bytes 884740
  52.8 42.5 %copy-start.18 = (f32[192]{0:T(256)S(1)}, f32[192]{0:T(256)}, u32[]{:S(2)}) copy-start(f32[192]{0:T(256)} %param.15) | copy-start | bytes 2308
  82.7 1.5 copy-start.2
  82.7 2.2 copy-start.5
  101.7 71.5 %copy-start.17 = (f32[768]{0:T(1024)S(1)}, f32[768]{0:T(1024)}, u32[]{:S(2)}) copy-start(f32[768]{0:T(1024)} %param.17) | copy-start | bytes 9220
  101.7 105.9 %all-gather.7.cloned.1.call-start = ((), (), s32[]{:S(2)}) async-start(), calls=%async_computation.6 | async-start | bytes 4915200 | tf_op jit(solution)/shard_map/all_gather | solution.py:309
  174.4 68.2 %all-gather.9.cloned.1.call-start = ((), (), s32[]{:S(2)}) async-start(), calls=%async_computation.8 | async-start | bytes 4915200 | tf_op jit(solution)/shard_map/all_gather | solution.py:288
  175.0 67.6 %copy-start.19 = (f32[768]{0:T(1024)S(1)}, f32[768]{0:T(1024)}, u32[]{:S(2)}) copy-start(f32[768]{0:T(1024)} %param.19) | copy-start | bytes 9220
  175.0 178.8 %reduce-scatter.9.cloned.1.call-start = ((), (), s32[]{:S(2)}) async-start(), calls=%async_computation.9 | async-start | bytes 9830400 | tf_op jit(solution)/shard_map/reduce_scatter | solution.py:344
  266.0 12.2 %copy-start.24 = (bf16[768,768]{1,0:T(8,128)(2,1)S(1)}, bf16[768,768]{1,0:T(8,128)(2,1)}, u32[]{:S(2)}) copy-start(bf16[768,768]{1,0:T(8,128)(2,1)} %param.18) | copy-start | bytes 3538948
  276.1 2.0 copy-start.9
  283.7 115.4 %reduce-scatter.7.cloned.1.call-start = ((), (), s32[]{:S(2)}) async-start(), calls=%async_computation.7 | async-start | bytes 4915200 | tf_op jit(solution)/shard_map/reduce_scatter | solution.py:321
  292.6 106.5 %copy-start.10 = (bf16[640,768]{1,0:T(8,128)(2,1)S(1)}, bf16[640,768]{1,0:T(8,128)(2,1)}, u32[]{:S(2)}) copy-start(bf16[640,768]{1,0:T(8,128)(2,1)} %param.21) | copy-start | bytes 2949124
  292.6 143.4 %all-gather.11.cloned.1.call-start = ((), (), s32[]{:S(2)}) async-start(), calls=%async_computation.10 | async-start | bytes 4915200 | tf_op jit(solution)/shard_map/all_gather | solution.py:349
  402.9 153.3 %reduce-scatter.11.cloned.1.call-start = ((), (), s32[]{:S(2)}) async-start(), calls=%async_computation.11 | async-start | bytes 4915200 | tf_op jit(solution)/shard_map/reduce_scatter | solution.py:368
  457.8 41.3 %copy-start.26 = (bf16[768,576]{0,1:T(8,128)(2,1)S(1)}, bf16[768,576]{0,1:T(8,128)(2,1)}, u32[]{:S(2)}) copy-start(bf16[768,576]{0,1:T(8,128)(2,1)} %param.14) | copy-start | bytes 2654212
  506.3 288.8 %all-reduce.8.cloned.1.call-start = ((), (), s32[]{:S(2)}) async-start(), calls=%async_computation.12 | async-start | bytes 14155776 | tf_op jit(solution)/shard_map/psum | solution.py:377
  506.6 8.1 %copy-start.22 = (bf16[2560,768]{1,0:T(8,128)(2,1)S(1)}, bf16[2560,768]{1,0:T(8,128)(2,1)}, u32[]{:S(2)}) copy-start(bf16[2560,768]{1,0:T(8,128)(2,1)} %all-gather.9.cloned.1.call-done) | copy-start | bytes 11796484
  514.8 9.1 %copy-start.3 = (f32[2560,192]{1,0:T(8,128)S(1)}, f32[2560,192]{1,0:T(8,128)}, u32[]{:S(2)}) copy-start(f32[2560,192]{1,0:T(8,128)} %copy-done.2) | copy-start | bytes 5898244
  514.8 9.1 %copy-start.23 = (bf16[2560,768]{1,0:T(8,128)(2,1)S(1)}, bf16[2560,768]{1,0:T(8,128)(2,1)}, u32[]{:S(2)}) copy-start(bf16[2560,768]{1,0:T(8,128)(2,1)} %all-gather.11.cloned.1.call-done) | copy-start | bytes 11796484
  523.8 2.7 copy-start.11
  523.8 3.3 copy-start.21
  530.9 0.7 copy-start.20
  530.9 25.3 %copy-start.7 = (bf16[640,768]{1,0:T(8,128)(2,1)S(1)}, bf16[640,768]{1,0:T(8,128)(2,1)}, u32[]{:S(2)}) copy-start(bf16[640,768]{1,0:T(8,128)(2,1)} %param.11) | copy-start | bytes 2949124
  530.9 25.3 %copy-start.16 = (f32[768]{0:T(1024)S(1)}, f32[768]{0:T(1024)}, u32[]{:S(2)}) copy-start(f32[768]{0:T(1024)} %param.13) | copy-start | bytes 9220
  530.9 67.5 %copy-start.8 = (f32[640,768]{1,0:T(8,128)S(1)}, f32[640,768]{1,0:T(8,128)}, u32[]{:S(2)}) copy-start(f32[640,768]{1,0:T(8,128)} %get-tuple-element.51) | copy-start | bytes 5898244
  795.1 3.0 copy-start.14
  795.1 3.8 copy-start.13
  795.1 5.2 copy-start.12
  798.1 3.6 copy-start.1
Sparse Core Ops, SparseCore 0:
  11.6 35.6 all-gather.4
  101.8 69.1 reduce-scatter.4
  174.6 33.0 all-gather.6
  209.1 33.5 all-gather.8
  283.8 69.9 reduce-scatter.8
  356.2 42.8 reduce-scatter.6
  403.0 32.9 all-gather.10
  506.5 46.2 reduce-scatter.10
  558.4 236.7 all-reduce.7

commit v2 on v1

--- a/solution.py
+++ b/solution.py
@@ -261,10 +261,6 @@
     )(lengths, packed, att, lse, d_att)
 
 
-def ffn_totals(grad_up, grad_down, grad_hidden):
-    return lax.psum((grad_up, grad_down, grad_hidden), "dp")
-
-
 def local(
     tokens,
     lengths,
@@ -278,117 +274,100 @@
     down_weight,
     out_grad,
 ):
-    tensor_size = lax.axis_size("tensor")
-    own_rows = tokens.shape[0]
-    group_rows = own_rows * tensor_size
+    parts = lax.axis_size("tensor")
+    own_rows, width = tokens.shape
+    group_rows = own_rows * parts
+    head_width = attn_gain.shape[0]
+
+    def gather(values):
+        return lax.all_gather(values, "tensor", axis=0, tiled=True)
+
+    def to_rows(values):
+        blocks = values.reshape(parts, own_rows, head_width)
+        moved = lax.all_to_all(blocks, "tensor", 0, 0, tiled=True)
+        return moved.transpose(1, 0, 2).reshape(own_rows, width)
+
+    def to_heads(values):
+        blocks = values.reshape(own_rows, parts, head_width).transpose(1, 0, 2)
+        return lax.all_to_all(blocks, "tensor", 0, 0, tiled=True).reshape(group_rows, head_width)
+
     residual = tokens.astype(jnp.float32)
     in_unit, in_scale, in_normed = normalize(residual, in_gain)
-    gathered_in, gathered_grad = (
-        lax.all_gather(in_normed.astype(jnp.bfloat16), "tensor", axis=0, tiled=True),
-        lax.all_gather(out_grad, "tensor", axis=0, tiled=True),
-    )
+    gathered_in = gather(in_normed.astype(jnp.bfloat16))
+    full_out, full_up, full_down = gather(out_weight), gather(up_weight), gather(down_weight)
+    full_gains = gather(jnp.concatenate((attn_gain, hidden_gain))).reshape(parts, -1)
+    full_attn_gain = full_gains[:, :head_width].reshape(-1)
+    full_hidden_gain = full_gains[:, head_width:].reshape(-1)
+    full_up = full_up.reshape(parts, width, -1)
     packed = jnp.dot(gathered_in, qkv_weight, preferred_element_type=jnp.float32).astype(
         jnp.bfloat16
     )
     attended, log_total = attn_fwd(packed, lengths, 512, 512)
-    att_sum, att_square = lax.psum(
-        (jnp.sum(attended, axis=1), jnp.sum(attended * attended, axis=1)), "tensor"
-    )
-    att_mean = att_sum / D
-    att_scale = lax.rsqrt(att_square / D - att_mean * att_mean + EPS)
-    att_unit = (attended - att_mean[:, None]) * att_scale[:, None]
-    att_low = (att_unit * attn_gain).astype(jnp.bfloat16)
-    middle = residual + lax.psum_scatter(
-        jnp.dot(att_low, out_weight, preferred_element_type=jnp.float32),
-        "tensor",
-        scatter_dimension=0,
-        tiled=True,
-    )
+    own_att = to_rows(attended.astype(jnp.bfloat16)).astype(jnp.float32)
+
+    att_unit, att_scale, att_normed = normalize(own_att, full_attn_gain)
+    att_low = att_normed.astype(jnp.bfloat16)
+    middle = residual + jnp.dot(att_low, full_out, preferred_element_type=jnp.float32)
     mid_unit, mid_scale, mid_normed = normalize(middle, ffn_gain)
     mid_low = mid_normed.astype(jnp.bfloat16)
-    gathered_mid = lax.all_gather(mid_low, "tensor", axis=0, tiled=True)
-    pre_act = jnp.dot(gathered_mid, up_weight, preferred_element_type=jnp.float32)
+    pre_act = jnp.einsum("rk,tkn->rtn", mid_low, full_up, preferred_element_type=jnp.float32)
+    pre_act = pre_act.reshape(own_rows, -1)
     activated, gelu_pull = jax.vjp(partial(jax.nn.gelu, approximate=True), pre_act)
-    act_sum, act_square = lax.psum(
-        (jnp.sum(activated, axis=1), jnp.sum(activated * activated, axis=1)), "tensor"
-    )
-    act_mean = act_sum / FF
-    act_scale = lax.rsqrt(act_square / FF - act_mean * act_mean + EPS)
-    act_unit = (activated - act_mean[:, None]) * act_scale[:, None]
-    act_low = (act_unit * hidden_gain).astype(jnp.bfloat16)
-    result = (
-        middle
-        + lax.psum_scatter(
-            jnp.dot(
-                lax.slice_in_dim(act_low, 0, lax.axis_size("tensor") * own_rows, axis=0),
-                down_weight,
-                preferred_element_type=jnp.float32,
-            ).astype(jnp.bfloat16),
-            "tensor",
-            scatter_dimension=0,
-            tiled=True,
-        ).astype(jnp.float32)
-    ).astype(jnp.bfloat16)
-    grad_down = contract_rows(act_low, gathered_grad)
-    grad_act_low = contract_cols(gathered_grad, down_weight)
-    weighted_act = grad_act_low * hidden_gain
-    grad_hidden = jnp.sum(grad_act_low * act_unit, axis=0)
-    first_sum, second_sum = lax.psum(
-        (jnp.sum(weighted_act, axis=1), jnp.sum(weighted_act * act_unit, axis=1)), "tensor"
-    )
-    grad_act = act_scale[:, None] * (
-        weighted_act - (first_sum / FF)[:, None] - act_unit * (second_sum / FF)[:, None]
-    )
-    grad_pre = gelu_pull(grad_act)[0].astype(jnp.bfloat16)
-    grad_up = contract_rows(gathered_mid, grad_pre)
-    grad_mid_normed = lax.psum_scatter(
-        contract_cols(grad_pre, up_weight), "tensor", scatter_dimension=0, tiled=True
-    )
-    grad_mid_part, grad_ffn_gain_part = norm_back(grad_mid_normed, mid_unit, mid_scale, ffn_gain)
+    act_unit, act_scale, act_normed = normalize(activated, full_hidden_gain)
+    act_low = act_normed.astype(jnp.bfloat16)
+    result = (middle + jnp.dot(act_low, full_down, preferred_element_type=jnp.float32)).astype(
+        jnp.bfloat16
+    )
+    grad_down = contract_rows(act_low, out_grad)
+    grad_act_low = contract_cols(out_grad, full_down)
+    grad_act, grad_hidden = norm_back(grad_act_low, act_unit, act_scale, full_hidden_gain)
+    grad_pre = gelu_pull(grad_act)[0].astype(jnp.bfloat16).reshape(own_rows, parts, -1)
+    grad_up = jnp.einsum("rk,rtn->tkn", mid_low, grad_pre, preferred_element_type=jnp.float32)
+    grad_mid_normed = jnp.einsum(
+        "rtn,tkn->rk", grad_pre, full_up, preferred_element_type=jnp.float32
+    )
+    grad_mid_part, grad_ffn_gain = norm_back(grad_mid_normed, mid_unit, mid_scale, ffn_gain)
     grad_middle = out_grad.astype(jnp.float32) + grad_mid_part
-    gathered_back = lax.all_gather(grad_middle.astype(jnp.bfloat16), "tensor", axis=0, tiled=True)
-    grad_out_part = contract_rows(att_low, gathered_back)
-    grad_att_low = contract_cols(gathered_back, out_weight)
-    weighted_att = grad_att_low * attn_gain
-    grad_attn_gain_part = jnp.sum(grad_att_low * att_unit, axis=0)
-    first_att, second_att, grad_ffn_gain_group = lax.psum(
-        (
-            jnp.sum(weighted_att, axis=1),
-            jnp.sum(weighted_att * att_unit, axis=1),
-            grad_ffn_gain_part,
-        ),
-        "tensor",
-    )
-    grad_attended = (
-        att_scale[:, None]
-        * (weighted_att - (first_att / D)[:, None] - att_unit * (second_att / D)[:, None])
-    ).astype(jnp.bfloat16)
+    grad_mid_low = grad_middle.astype(jnp.bfloat16)
+    grad_out = contract_rows(att_low, grad_mid_low)
+    grad_att_low = contract_cols(grad_mid_low, full_out)
+    grad_att, grad_attn_gain = norm_back(grad_att_low, att_unit, att_scale, full_attn_gain)
+    grad_attended = to_heads(grad_att.astype(jnp.bfloat16))
+
+    def scatter(values):
+        return lax.psum_scatter(
+            values.astype(jnp.bfloat16), "tensor", scatter_dimension=0, tiled=True
+        )
+
+    def total(values):
+        return lax.psum(values, "dp")
+
+    down_sum = total(scatter(grad_down).astype(jnp.float32))
+    up_sum = total(scatter(grad_up.reshape(parts * width, -1)).astype(jnp.float32))
+    out_sum = total(scatter(grad_out).astype(jnp.float32))
+
     grad_packed = attn_bwd(packed, lengths, attended, log_total, grad_attended, 512, 256)
-    grad_qkv_part = contract_rows(gathered_in, grad_packed)
-    grad_in_normed = lax.psum_scatter(
-        contract_cols(grad_packed, qkv_weight).astype(jnp.bfloat16),
-        "tensor",
-        scatter_dimension=0,
-        tiled=True,
-    ).astype(jnp.float32)
-    grad_in_part, grad_in_gain_part = norm_back(grad_in_normed, in_unit, in_scale, in_gain)
+    qkv_sum = total(contract_rows(gathered_in, grad_packed))
+    grad_in_normed = scatter(contract_cols(grad_packed, qkv_weight)).astype(jnp.float32)
+    grad_in_part, grad_in_gain = norm_back(grad_in_normed, in_unit, in_scale, in_gain)
     in_grad = grad_middle + grad_in_part
-    ffn_sums = ffn_totals(grad_up, grad_down, grad_hidden)
-    attn_sums = lax.psum(
-        (grad_qkv_part, grad_out_part, grad_attn_gain_part, grad_ffn_gain_group), "dp"
-    )
-    grad_in_gain = lax.psum(grad_in_gain_part, ("dp", "tensor"))
+    gains = lax.psum(
+        jnp.concatenate((grad_in_gain, grad_ffn_gain, grad_attn_gain, grad_hidden)),
+        ("dp", "tensor"),
+    )
+    me = lax.axis_index("tensor")
+    hidden = hidden_gain.shape[0]
     return (
         result,
         in_grad,
-        grad_in_gain,
-        attn_sums[0],
-        attn_sums[2],
-        attn_sums[1],
-        attn_sums[3],
-        ffn_sums[0],
-        ffn_sums[2],
-        ffn_sums[1],
+        gains[:width],
+        qkv_sum,
+        lax.dynamic_slice_in_dim(gains, 2 * width + me * head_width, head_width),
+        out_sum,
+        gains[width : 2 * width],
+        up_sum,
+        lax.dynamic_slice_in_dim(gains, 3 * width + me * hidden, hidden),
+        down_sum,
     )
 
 

time: 818 us -> 656 us (0.80)
  waiting for transfers between devices: 482 us -> 124 us
  blocking collectives: 108 us -> 320 us
  Pallas kernels: 71.2 us -> 58.8 us
  local copies, waits for them, and re-layouts: 11.4 us -> 22.1 us
  other arithmetic: 36 us -> 26.4 us
    psum x1, waiting for transfers between devices: 194 us -> 0.01 us  [total(): return lax.psum(values, 'dp')]
    psum x6 -> x2, blocking collectives: 108 us -> 266 us  [the longest x1 226 us: total(): return lax.psum(values, 'dp')]
    reduce_scatter x4, waiting for transfers between devices: 173 us -> 72.7 us  [scatter(): lax.psum_scatter(values.astype(jnp.bfloat16), 'tensor', scatter_dimension...]
    all_gather x4, waiting for transfers between devices: 115 us -> 49.3 us  [gather(): return lax.all_gather(values, 'tensor', axis=0, tiled=True)]
    unnamed x0 -> x1, blocking collectives: none -> 29.4 us
    all_to_all x0 -> x1, blocking collectives: none -> 24.6 us  [to_heads(): lax.all_to_all(blocks, 'tensor', 0, 0, tiled=True)]
    dot_general x3 -> x5, matrix products: 24.5 us -> 35.3 us  [the longest x1 10.1 us: local(): jnp.einsum('rk,tkn->rtn', mid_low, full_up, preferred_element_type=jnp.fl...]
    dot_general x4 -> x3, matrix products: 30.3 us -> 19.9 us  [contract_cols(): lax.dot_general(left, right, (((1,), (1,)), ((), ())), preferred_element_...]
  transfers between devices with their start and end apart: 9 -> 10, of which waited for: 8 -> 5; matrix products, arithmetic and copies ran while one was open for 6% -> 14% of each run, Pallas kernels for 0% -> 9%
where the time goes in v2:
time: 656 us; the launch traced here: 650 us
  blocking collectives  320 us (49%)
  waiting for transfers between devices  124 us (19%)
  matrix products  78.9 us (12%)
  Pallas kernels  58.8 us (9%)
  other arithmetic  26.4 us (4%)
  local copies, waits for them, and re-layouts  22.1 us (3%)
  between operations  15.4 us (2%)
    psum x1, blocking collectives, total(): return lax.psum(values, 'dp')  226 us
    reduce_scatter x4, waiting for transfers between devices, scatter(): lax.psum_scatter(values.astype(jnp.bfloat16), 'tensor', scatter_dimension...  72.7 us
    all_gather x4, waiting for transfers between devices, gather(): return lax.all_gather(values, 'tensor', axis=0, tiled=True)  49.3 us
    psum x1, blocking collectives, local(): lax.psum(jnp.concatenate((grad_in_gain, grad_ffn_gain, grad_attn_gain, gr...  39.8 us
    pallas_call x1, Pallas kernels, attn_bwd(): pl.pallas_call(partial(bwd_kernel, bq, bk), out_shape=jax.ShapeDtypeStruc...  36.2 us
    unnamed x1, blocking collectives  29.4 us
    all_to_all x1, blocking collectives, to_heads(): lax.all_to_all(blocks, 'tensor', 0, 0, tiled=True)  24.6 us
    pallas_call x1, Pallas kernels, attn_fwd(): pl.pallas_call(partial(fwd_kernel, bq, bk), out_shape=(jax.ShapeDtypeStru...  22.5 us
  transfers between devices with their start and end apart: 10, of which 5 were waited for; matrix products, arithmetic and copies ran while one was open for 14% of the time, Pallas kernels for 9%

profile of v2, /device:TPU:0, one launch (start us, length us, event | category | flops | bytes accessed | tf_op | source)
XLA Modules:
  0.0 649.6 jit_solution(5077718936760599059)
XLA Ops:
  7.2 1.7 convert_reduce_fusion
  8.9 2.5 fusion.27
  11.5 0.7 all-gather.7.cloned.1.call-update
  12.2 0.7 all-gather.9.cloned.1.call-update
  13.0 0.5 all-gather.11.cloned.1.call-update
  13.5 33.8 %all-gather.5.cloned.1.call-done = bf16[2560,768]{1,0:T(8,128)(2,1)} async-done(((bf16[640,768]{1,0:T(8,128)(2,1)}), bf16[2560,768]{1,0:T(8,128)(2,1)}) %all-gather.5.cloned.1.call-update) | async-done | bytes 3932176 | tf_op jit(solution)/shard_map/all_gather | solution.py:283
  47.3 5.4 convolution_convert_fusion.2.qkv_ref
  52.7 22.5 %attn_fwd.1 = (f32[2560,192]{1,0:T(8,128)S(1)}, f32[8,2560]{1,0:T(8,128)S(1)}) custom-call(s32[1,5]{1,0:T(1,128)S(1)} %copy-done.4, bf16[2560,576]{1,0:T(8,128)(2,1)S(1)} %convolution_convert_fusion.2.qkv_ref), custom_call_target="tpu_custom_call" | custom-call | tf_op jit(solution)/shard_map/attn_fwd/pallas_call | solution.py:143
  75.4 1.3 copy-done.2
  76.7 1.3 copy.28
  78.1 3.5 all-to-all-start
  81.7 0.6 dynamic-slice
  83.1 29.4 %all-reduce = f32[3840]{0:T(1024)S(1)} all-reduce(f32[3840]{0:T(1024)S(1)} %maximum_dynamic-update-slice_fusion), channel_id=1, replica_groups=mesh['dp'=8,'tensor'=4] {'tensor'}, use_global_device_ids=true, to_apply=%add | all-reduce | flops 3840 | bytes 30720
  112.8 1.5 convert_element_type.107
  114.4 1.9 copy.29
  116.3 2.2 convert_reduce_fusion.1
  118.5 3.9 fusion.37
  122.5 7.0 %copy.30 = bf16[4,768,768]{2,1,0:T(8,128)(2,1)} copy(bf16[4,768,768]{1,2,0:T(8,128)(2,1)} %bitcast.61) | data formatting | bytes 9437184 | tf_op jit(solution)/shard_map/rk,tkn->rtn/dot_general | solution.py:313
  129.5 10.1 %fusion.36 = (f32[640]{0:T(1024)S(1)}, f32[640]{0:T(1024)S(1)}, f32[640,3072]{1,0:T(8,128)}) fusion(bf16[3072,768]{1,0:T(8,128)(2,1)} %bitcast.66, f32[640,768]{1,0:T(8,128)S(1)} %copy-done.10, f32[768]{0:T(1024)S(1)} %copy-done.15, f32[640]{0:T(1024)S(1)} %get-tuple-element.45, f32[640]{0:T(1024)S(1)} %get-tuple-element.44), kind=kOutput, calls=%fused_computation.87 | convolution fusion | flops 3043490816 | bytes 14562304 | tf_op jit(solution)/shard_map/rk,tkn->rtn/dot_general | solution.py:313
  139.6 15.5 %all-gather.11.cloned.1.call-done = bf16[3072,768]{1,0:T(8,128)(2,1)} async-done(((bf16[768,768]{1,0:T(8,128)(2,1)}), bf16[3072,768]{1,0:T(8,128)(2,1)}) %all-gather.11.cloned.1.call-update) | async-done | bytes 4718608 | tf_op jit(solution)/shard_map/all_gather | solution.py:283
  155.0 9.5 %multiply_reduce_fusion = (f32[3072]{0:T(1024)S(1)}, f32[640]{0:T(1024)S(1)}, f32[640]{0:T(1024)S(1)}, f32[640,3072]{1,0:T(8,128)S(1)}) fusion(f32[640]{0:T(1024)S(1)} %get-tuple-element.43, f32[640]{0:T(1024)S(1)} %get-tuple-element.42, f32[640,3072]{1,0:T(8,128)} %get-tuple-element.51, f32[3072]{0:T(1024)S(1)} %mul.295, bf16[640,768]{1,0:T(8,128)(2,1)} %param.21, ...), kind=kOutput, calls=%fused_computation.9 | convolution fusion | flops 3051352064 | bytes 21465088 | tf_op jit(solution)/shard_map/dot_general | solution.py:26
  164.6 9.8 %fusion.6 = (bf16[640,3072]{1,0:T(8,128)(2,1)S(1)}, bf16[640,3072]{1,0:T(8,128)(2,1)}) fusion(f32[640,3072]{1,0:T(8,128)S(1)} %bitcast.58, f32[640,3072]{1,0:T(8,128)S(1)} %get-tuple-element.52, f32[640]{0:T(1024)S(1)} %get-tuple-element.55, f32[640]{0:T(1024)S(1)} %get-tuple-element.56, f32[3072]{0:T(1024)S(1)} %mul.295, f32[640]{0:T(1024)S(1)} %get-tuple-element.43, ...), kind=kLoop, calls=%fused_computation.8 | loop fusion | flops 58982400 | bytes 23615488 | tf_op jit(solution)/shard_map/convert_element_type | solution.py:324
  174.5 3.6 fusion.29
  178.2 0.7 multiply_add_fusion
  178.9 0.8 copy-done.6
  179.7 2.4 convolution_convert_fusion.3
  182.2 3.3 multiply_reduce_fusion.4
  185.6 1.5 multiply_convert_fusion.1
  187.1 2.3 copy.32
  189.3 24.6 %all_to_all.10 = bf16[4,640,192]{1,2,0:T(8,128)(2,1)} all-to-all(bf16[4,640,192]{1,2,0:T(8,128)(2,1)} %bitcast.69), channel_id=1, replica_groups=mesh['dp'=8,'tensor'=4] {'tensor'}, dimensions={0} | all-to-all | bytes 1966080 | tf_op jit(solution)/shard_map/all_to_all | solution.py:292
  213.9 2.4 copy.33
  216.3 36.2 %attn_bwd.1 = bf16[2560,576]{1,0:T(8,128)(2,1)} custom-call(s32[1,5]{1,0:T(1,128)} %len_ref.3, bf16[2560,576]{1,0:T(8,128)(2,1)} %copy-done.1, f32[2560,192]{1,0:T(8,128)} %copy-done.2, f32[8,2560]{1,0:T(8,128)} %copy-done.3, bf16[2560,192]{1,0:T(8,128)(2,1)} %bitcast.60), custom_call_target="tpu_custom_call" | custom-call | tf_op jit(solution)/shard_map/attn_bwd/pallas_call | solution.py:248
  252.5 7.1 %convolution_convert_fusion.1 = bf16[2560,768]{1,0:T(8,128)(2,1)} fusion(bf16[2560,576]{1,0:T(8,128)(2,1)} %attn_bwd.1, bf16[768,576]{0,1:T(8,128)(2,1)S(1)} %copy-done), kind=kOutput, calls=%fused_computation.17 | convolution fusion | flops 2266890240 | bytes 7766016 | tf_op jit(solution)/shard_map/dot_general | solution.py:26
  259.7 8.8 %fusion.13 = bf16[4,768,768]{1,2,0:T(8,128)(2,1)} fusion(bf16[80,4,8,768]{3,2,1,0:T(8,128)(2,1)} %bitcast.68, f32[640,768]{1,0:T(8,128)} %get-tuple-element.50, f32[768]{0:T(1024)S(1)} %copy-done.15, f32[640]{0:T(1024)S(1)} %get-tuple-element.45, f32[640]{0:T(1024)S(1)} %get-tuple-element.44), kind=kOutput, calls=%fused_computation.29 | convolution fusion | flops 3024224256 | bytes 10625024 | tf_op jit(solution)/shard_map/rk,rtn->tkn/dot_general | solution.py:325
  268.5 0.3 reduce-scatter.11.cloned.1.call-start
  268.8 8.5 %convolution_convert_fusion = bf16[3072,768]{1,0:T(8,128)(2,1)} fusion(bf16[640,3072]{1,0:T(8,128)(2,1)} %get-tuple-element.38, bf16[640,768]{1,0:T(8,128)(2,1)} %param.21), kind=kOutput, calls=%fused_computation.16 | convolution fusion | flops 3022258176 | bytes 9633792 | tf_op jit(solution)/shard_map/dot_general | solution.py:20
  277.4 7.5 %fusion.39 = f32[768,576]{0,1:T(8,128)} fusion(bf16[2560,768]{1,0:T(8,128)(2,1)} %all-gather.5.cloned.1.call-done, bf16[2560,576]{1,0:T(8,128)(2,1)} %attn_bwd.1), kind=kOutput, calls=%fused_computation.90 | convolution fusion | flops 2264924160 | bytes 8650752 | tf_op jit(solution)/shard_map/dot_general | solution.py:20
  284.9 8.9 %add_convert_fusion = bf16[640,768]{1,0:T(8,128)(2,1)} fusion(f32[640,768]{1,0:T(8,128)} %get-tuple-element.50, bf16[640,3072]{1,0:T(8,128)(2,1)} %get-tuple-element.38, bf16[3072,768]{1,0:T(8,128)(2,1)} %all-gather.11.cloned.1.call-done), kind=kOutput, calls=%fused_computation.53 | convolution fusion | flops 3020881920 | bytes 11599872 | tf_op jit(solution)/shard_map/dot_general | solution.py:318
  293.8 18.2 %reduce-scatter.5.cloned.1.call-done = bf16[640,768]{1,0:T(8,128)(2,1)} async-done(((bf16[2560,768]{1,0:T(8,128)(2,1)}), bf16[640,768]{1,0:T(8,128)(2,1)}) %reduce-scatter.5.cloned.1.call-update) | async-done | bytes 983056 | tf_op jit(solution)/shard_map/reduce_scatter | solution.py:338
  312.1 2.5 fusion.23
  314.6 39.8 %psum.35 = f32[5376]{0:T(1024)S(1)} all-reduce(f32[5376]{0:T(1024)S(1)} %pad_maximum_fusion), channel_id=1, replica_groups=mesh['dp'=8,'tensor'=4] {'dp','tensor'}, use_global_device_ids=true, to_apply=%region_21.0 | all-reduce | flops 5376 | bytes 43008 | tf_op jit(solution)/shard_map/psum | solution.py:354
  354.4 0.6 dynamic_slice.6
  355.1 0.7 fusion.38
  355.7 3.5 fusion.21
  359.3 3.9 reduce-scatter.9.cloned.1.call-done
  363.1 50.5 %reduce-scatter.11.cloned.1.call-done = bf16[768,768]{1,0:T(8,128)(2,1)} async-done(((bf16[3072,768]{1,0:T(8,128)(2,1)}), bf16[768,768]{1,0:T(8,128)(2,1)}) %reduce-scatter.11.cloned.1.call-update) | async-done | bytes 1179664 | tf_op jit(solution)/shard_map/reduce_scatter | solution.py:338
  413.7 226.1 %all-reduce.6 = (f32[192,768]{1,0:T(8,128)}, f32[768,768]{1,0:T(8,128)}, f32[768,768]{1,0:T(8,128)}) all-reduce(bf16[192,768]{1,0:T(8,128)(2,1)S(1)} %copy-done.13, bf16[768,768]{1,0:T(8,128)(2,1)} %reduce-scatter.9.cloned.1.call-done, bf16[768,768]{1,0:T(8,128)(2,1)} %reduce-scatter.11.cloned.1.call-done), channel_id=1, replica_groups=mesh['dp'=8,'tensor'=4] {'dp'}, use_global_device_ids=true, to_apply=%region_24.0 | all-reduce | flops 1327104 | bytes 7962624 | tf_op jit(solution)/shard_map/psum | solution.py:343
  639.8 2.8 copy.60
  (85 shorter events, 1.3 us)
Async XLA Ops:
  7.2 40.1 %copy-start = (bf16[768,576]{0,1:T(8,128)(2,1)S(1)}, bf16[768,576]{0,1:T(8,128)(2,1)}, u32[]{:S(2)}) copy-start(bf16[768,576]{0,1:T(8,128)(2,1)} %param.14) | copy-start | bytes 2654212
  7.2 40.1 %all-gather.5.cloned.1.call-start = ((), (), s32[]{:S(2)}) async-start(), calls=%async_computation.6 | async-start | bytes 4915200 | tf_op jit(solution)/shard_map/all_gather | solution.py:283
  11.4 107.1 %all-gather.7.cloned.1.call-start = ((), (), s32[]{:S(2)}) async-start(), calls=%async_computation.7 | async-start | bytes 1474560 | tf_op jit(solution)/shard_map/all_gather | solution.py:283
  12.2 110.2 %all-gather.9.cloned.1.call-start = ((), (), s32[]{:S(2)}) async-start(), calls=%async_computation.8 | async-start | bytes 5898240 | tf_op jit(solution)/shard_map/all_gather | solution.py:283
  12.9 142.1 %all-gather.11.cloned.1.call-start = ((), (), s32[]{:S(2)}) async-start(), calls=%async_computation.9 | async-start | bytes 5898240 | tf_op jit(solution)/shard_map/all_gather | solution.py:283
  13.5 39.2 %copy-start.4 = (s32[1,5]{1,0:T(1,128)S(1)}, s32[1,5]{1,0:T(1,128)}, u32[]{:S(2)}) copy-start(s32[1,5]{1,0:T(1,128)} %len_ref.3) | copy-start | bytes 64
  52.7 22.7 %copy-start.1 = (bf16[2560,576]{1,0:T(8,128)(2,1)}, bf16[2560,576]{1,0:T(8,128)(2,1)S(1)}, u32[]{:S(2)}) copy-start(bf16[2560,576]{1,0:T(8,128)(2,1)S(1)} %convolution_convert_fusion.2.qkv_ref) | copy-start | bytes 8847364
  75.2 1.5 copy-start.2
  75.2 1.5 copy-start.3
  76.7 4.9 copy-start.18
  76.7 6.2 copy-start.16
  76.7 6.2 copy-start.17
  78.1 34.7 %all-to-all-start = ((bf16[4,640,192]{1,2,0:T(8,128)(2,1)}), bf16[4,640,192]{1,2,0:T(8,128)(2,1)S(1)}, u32[]{:S(2)}, u32[]{:S(2)}) async-start(bf16[4,640,192]{1,2,0:T(8,128)(2,1)} %copy.28), calls=%async_computation | async-start | bytes 1966080 | tf_op jit(solution)/shard_map/all_to_all | solution.py:287
  81.6 212.2 %reduce-scatter.7.cloned.1.call-start = ((), (), s32[]{:S(2)}) async-start(), calls=%async_computation.12 | async-start | bytes 1474560 | tf_op jit(solution)/shard_map/reduce_scatter | solution.py:338
  112.8 1.6 copy-start.8
  116.2 6.2 copy-start.5
  122.4 7.1 %copy-start.10 = (f32[640,768]{1,0:T(8,128)S(1)}, f32[640,768]{1,0:T(8,128)}, u32[]{:S(2)}) copy-start(f32[640,768]{1,0:T(8,128)} %get-tuple-element.50) | copy-start | bytes 5898244
  122.5 7.0 %copy-start.15 = (f32[768]{0:T(1024)S(1)}, f32[768]{0:T(1024)}, u32[]{:S(2)}) copy-start(f32[768]{0:T(1024)} %param.17) | copy-start | bytes 9220
  129.5 44.9 %slice-start.2 = ((s8[4718592]{0:T(1024)(128)(4,1)}), s8[524288]{0:T(1024)(128)(4,1)S(1)}, s32[]{:S(2)}) async-start(s8[4718592]{0:T(1024)(128)(4,1)} %bitcast.62), calls=%async_computation.17 | async-start | bytes 1048576
  155.0 9.5 %slice-start = ((s8[7864320]{0:T(1024)(128)(4,1)}), s8[4194304]{0:T(1024)(128)(4,1)S(1)}, s32[]{:S(2)}) async-start(s8[7864320]{0:T(1024)(128)(4,1)} %bitcast.57), calls=%async_computation.15 | async-start | bytes 8388608
  155.0 9.5 %slice-start.1 = ((s8[7864320]{0:T(1024)(128)(4,1)}), s8[3670016]{0:T(1024)(128)(4,1)S(1)}, s32[]{:S(2)}) async-start(s8[7864320]{0:T(1024)(128)(4,1)} %bitcast.57), calls=%async_computation.16 | async-start | bytes 7340032
  155.0 19.4 %slice-start.3 = ((s8[4718592]{0:T(1024)(128)(4,1)}), s8[4194304]{0:T(1024)(128)(4,1)S(1)}, s32[]{:S(2)}) async-start(s8[4718592]{0:T(1024)(128)(4,1)} %bitcast.62), calls=%async_computation.18 | async-start | bytes 8388608
  174.4 3.7 copy-start.9
  174.5 3.7 copy-start.11
  174.5 3.7 copy-start.12
  178.1 1.5 copy-start.6
  182.1 129.9 %reduce-scatter.5.cloned.1.call-start = ((), (), s32[]{:S(2)}) async-start(), calls=%async_computation.10 | async-start | bytes 4915200 | tf_op jit(solution)/shard_map/reduce_scatter | solution.py:338
  182.2 3.4 copy-start.7
  259.6 103.5 %reduce-scatter.9.cloned.1.call-start = ((), (), s32[]{:S(2)}) async-start(), calls=%async_computation.13 | async-start | bytes 5898240 | tf_op jit(solution)/shard_map/reduce_scatter | solution.py:338
  268.5 145.1 %reduce-scatter.11.cloned.1.call-start = ((), (), s32[]{:S(2)}) async-start(), calls=%async_computation.14 | async-start | bytes 5898240 | tf_op jit(solution)/shard_map/reduce_scatter | solution.py:338
  277.3 362.5 %all-reduce.5.cloned.1.call-start = ((), (), s32[]{:S(2)}) async-start(), calls=%async_computation.11 | async-start | bytes 3538944 | tf_op jit(solution)/shard_map/psum | solution.py:343
  284.9 27.2 %copy-start.14 = (f32[768]{0:T(1024)S(1)}, f32[768]{0:T(1024)}, u32[]{:S(2)}) copy-start(f32[768]{0:T(1024)} %param.13) | copy-start | bytes 9220
  355.7 58.0 %copy-start.13 = (bf16[192,768]{1,0:T(8,128)(2,1)S(1)}, bf16[192,768]{1,0:T(8,128)(2,1)}, u32[]{:S(2)}) copy-start(bf16[192,768]{1,0:T(8,128)(2,1)} %reduce-scatter.7.cloned.1.call-done) | copy-start | bytes 884740
Sparse Core Ops, SparseCore 0:
  11.6 35.6 all-gather.4
  48.8 17.4 all-gather.6
  67.9 48.3 all-gather.8
  117.7 37.2 all-gather.10
  182.2 32.0 reduce-scatter.6
  259.7 52.2 reduce-scatter.4
  314.6 48.5 reduce-scatter.8
  365.8 47.7 reduce-scatter.10
  417.9 144.8 all-reduce.4

commit v3 on v2

--- a/solution.py
+++ b/solution.py
@@ -261,6 +261,221 @@
     )(lengths, packed, att, lse, d_att)
 
 
+MESH = pl.DeviceIdType.MESH
+CHUNK = 192
+
+
+def flip(index, bit):
+    return index + bit - 2 * bit * ((index // bit) % 2)
+
+
+def peers_of(parts, groups):
+    steps, bit = [], 1
+    while bit < parts:
+        steps.append(("tensor", bit))
+        bit *= 2
+    bit = 1
+    while bit < groups:
+        steps.append(("dp", bit))
+        bit *= 2
+    return steps
+
+
+def at_peer(axis, bit):
+    return {axis: flip(lax.axis_index(axis), bit)}
+
+
+def greet(steps):
+    barrier = pltpu.get_barrier_semaphore()
+    for axis, bit in steps:
+        pl.semaphore_signal(barrier, inc=1, device_id=at_peer(axis, bit), device_id_type=MESH)
+    pl.semaphore_wait(barrier, len(steps))
+
+
+def remote(src, dst, send, recv, axis, bit):
+    copy = pltpu.make_async_remote_copy(
+        src_ref=src,
+        dst_ref=dst,
+        send_sem=send,
+        recv_sem=recv,
+        device_id=at_peer(axis, bit),
+        device_id_type=MESH,
+    )
+    copy.start()
+    return copy
+
+
+def rounded(values):
+    return values.astype(jnp.bfloat16)
+
+
+def sync_kernel(groups, sizes, out_ref, up_ref, down_ref, gains_ref, sum_ref, gains_sum_ref,
+                own, first, second, acc, to_y, to_x, from_x, to_z, from_z, to_w, from_w,
+                more_to, more_from, gain_at, send, recv, local_sem, gain_send, gain_recv):
+    steps = peers_of(4, groups)
+    me, dp = lax.axis_index("tensor"), lax.axis_index("dp")
+    cols = out_ref.shape[1]
+    half, rows2, rows4 = cols // 2, CHUNK // 2, CHUNK // 4
+    b0, b1, b2 = dp % 2, (dp // 2) % 2, (dp // 4) % 2
+    chunks = []
+    for ref, size in zip((down_ref, up_ref, out_ref), sizes):
+        for at in range(0, size, CHUNK):
+            chunks.append((ref, size, at))
+    far = steps[5:]
+    flight = {}
+    sends = []
+
+    def take(ref, size, shard, at):
+        return ref.at[pl.ds(pl.multiple_of(shard * size + at, 16), CHUNK), :]
+
+    def go(c, s, src, dst, axis, bit):
+        copy = remote(src, dst, send.at[c, s], recv.at[c, s], axis, bit)
+        flight[c, s] = copy
+        sends.append(copy)
+
+    def col(b):
+        return pl.ds(pl.multiple_of(b * half, 128), half)
+
+    def row2(b):
+        return pl.ds(pl.multiple_of(b * rows2, 16), rows2)
+
+    def row4(b, bb):
+        return pl.ds(pl.multiple_of(b * rows2 + bb * rows4, 16), rows4)
+
+    def pair(c):
+        ref, size, at = chunks[c]
+        go(c, 0, take(ref, size, flip(me, 1), at), first.at[c, 0], "tensor", 1)
+        go(c, 1, take(ref, size, flip(flip(me, 1), 2), at), first.at[c, 1], "tensor", 1)
+        for k, shard in enumerate((me, flip(me, 2))):
+            copy = pltpu.make_async_copy(take(ref, size, shard, at), own.at[c, k], local_sem.at[c, k])
+            copy.start()
+            flight[c, "own", k] = copy
+
+    def chip(c):
+        flight[c, "own", 1].wait()
+        flight[c, 1].wait_recv()
+        to_y[c] = rounded(own[c, 1].astype(jnp.float32) + first[c, 1].astype(jnp.float32))
+        go(c, 2, to_y.at[c], second.at[c], "tensor", 2)
+        flight[c, "own", 0].wait()
+        flight[c, 0].wait_recv()
+        acc[c] = own[c, 0].astype(jnp.float32) + first[c, 0].astype(jnp.float32)
+
+    def x_half(c):
+        flight[c, 2].wait_recv()
+        acc[c] += second[c].astype(jnp.float32)
+        to_x[c] = rounded(acc[c, :, col(1 - b0)])
+        go(c, 3, to_x.at[c], from_x.at[c], "dp", 1)
+
+    def z_half(c):
+        flight[c, 3].wait_recv()
+        acc[c, :, col(b0)] += from_x[c].astype(jnp.float32)
+        to_z[c] = rounded(acc[c, row2(1 - b1), col(b0)])
+        go(c, 4, to_z.at[c], from_z.at[c], "dp", 2)
+
+    def z_quarter(c):
+        flight[c, 4].wait_recv()
+        acc[c, row2(b1), col(b0)] += from_z[c].astype(jnp.float32)
+        to_w[c] = rounded(acc[c, row4(b1, 1 - b2), col(b0)])
+        go(c, 5, to_w.at[c], from_w.at[c], "dp", 4)
+
+    def settle(c):
+        flight[c, 5].wait_recv()
+        mine = acc[c, row4(b1, b2), col(b0)] + from_w[c].astype(jnp.float32)
+        for n, (axis, bit) in enumerate(far):
+            more_to[c, n] = rounded(mine)
+            go(c, 9 + n, more_to.at[c, n], more_from.at[c, n], axis, bit)
+            flight[c, 9 + n].wait_recv()
+            mine = rounded(mine).astype(jnp.float32) + more_from[c, n].astype(jnp.float32)
+        sum_ref[c, row4(b1, b2), col(b0)] = rounded(mine)
+        piece = sum_ref.at[c, row4(b1, b2), col(b0)]
+        go(c, 6, piece, piece, "dp", 4)
+
+    def z_share(c):
+        flight[c, 6].wait_recv()
+        piece = sum_ref.at[c, row2(b1), col(b0)]
+        go(c, 7, piece, piece, "dp", 2)
+
+    def x_share(c):
+        flight[c, 7].wait_recv()
+        piece = sum_ref.at[c, :, col(b0)]
+        go(c, 8, piece, piece, "dp", 1)
+
+    def end(c):
+        flight[c, 8].wait_recv()
+
+    stages = (pair, chip, x_half, z_half, z_quarter, settle, z_share, x_share, end)
+
+    def gain_start(n):
+        axis, bit = steps[n]
+        copy = remote(gain_at.at[0, n], gain_at.at[1, n], gain_send.at[n], gain_recv.at[n], axis, bit)
+        flight["gain", n] = copy
+        sends.append(copy)
+
+    greet(steps)
+    gain_at[0, 0] = gains_ref[...]
+    gain_start(0)
+    gain_turn = 0
+    for turn in range(len(chunks) + len(stages) - 1):
+        for s in reversed(range(len(stages))):
+            if 0 <= turn - s < len(chunks):
+                stages[s](turn - s)
+        if gain_turn < len(steps):
+            flight["gain", gain_turn].wait_recv()
+            now = gain_at[0, gain_turn] + gain_at[1, gain_turn]
+            gain_turn += 1
+            if gain_turn < len(steps):
+                gain_at[0, gain_turn] = now
+                gain_start(gain_turn)
+            else:
+                gains_sum_ref[...] = now
+    for copy in sends:
+        copy.wait_send()
+
+
+def grad_sync(groups, grad_out, grad_up, grad_down, gains):
+    width = grad_out.shape[1]
+    sizes = tuple(g.shape[0] // 4 for g in (grad_down, grad_up, grad_out))
+    n = sum(sizes) // CHUNK
+    steps = len(peers_of(4, groups))
+    extra = max(steps - 5, 1)
+    bf16 = lambda *shape: pltpu.VMEM(shape, jnp.bfloat16)
+    anywhere, vmem = pl.BlockSpec(memory_space=pl.ANY), pl.BlockSpec(memory_space=pltpu.VMEM)
+    return pl.pallas_call(
+        partial(sync_kernel, groups, sizes),
+        out_shape=(
+            jax.ShapeDtypeStruct((n, CHUNK, width), jnp.bfloat16),
+            jax.ShapeDtypeStruct(gains.shape, jnp.float32),
+        ),
+        in_specs=[anywhere] * 3 + [vmem],
+        out_specs=[vmem, vmem],
+        scratch_shapes=[
+            bf16(n, 2, CHUNK, width),
+            bf16(n, 2, CHUNK, width),
+            bf16(n, CHUNK, width),
+            pltpu.VMEM((n, CHUNK, width), jnp.float32),
+            bf16(n, CHUNK, width),
+            bf16(n, CHUNK, width // 2),
+            bf16(n, CHUNK, width // 2),
+            bf16(n, CHUNK // 2, width // 2),
+            bf16(n, CHUNK // 2, width // 2),
+            bf16(n, CHUNK // 4, width // 2),
+            bf16(n, CHUNK // 4, width // 2),
+            bf16(n, extra, CHUNK // 4, width // 2),
+            bf16(n, extra, CHUNK // 4, width // 2),
+            pltpu.VMEM((2, steps) + gains.shape, jnp.float32),
+            pltpu.SemaphoreType.DMA((n, 9 + extra)),
+            pltpu.SemaphoreType.DMA((n, 9 + extra)),
+            pltpu.SemaphoreType.DMA((n, 2)),
+            pltpu.SemaphoreType.DMA((steps,)),
+            pltpu.SemaphoreType.DMA((steps,)),
+        ],
+        compiler_params=pltpu.CompilerParams(
+            collective_id=0, has_side_effects=True, vmem_limit_bytes=56 << 20
+        ),
+        name="grad_sync",
+    )(grad_out, grad_up, grad_down, gains)
+
+
 def local(
     tokens,
     lengths,
@@ -334,29 +549,29 @@
     grad_att, grad_attn_gain = norm_back(grad_att_low, att_unit, att_scale, full_attn_gain)
     grad_attended = to_heads(grad_att.astype(jnp.bfloat16))
 
-    def scatter(values):
-        return lax.psum_scatter(
-            values.astype(jnp.bfloat16), "tensor", scatter_dimension=0, tiled=True
-        )
-
-    def total(values):
-        return lax.psum(values, "dp")
-
-    down_sum = total(scatter(grad_down).astype(jnp.float32))
-    up_sum = total(scatter(grad_up.reshape(parts * width, -1)).astype(jnp.float32))
-    out_sum = total(scatter(grad_out).astype(jnp.float32))
-
     grad_packed = attn_bwd(packed, lengths, attended, log_total, grad_attended, 512, 256)
-    qkv_sum = total(contract_rows(gathered_in, grad_packed))
-    grad_in_normed = scatter(contract_cols(grad_packed, qkv_weight)).astype(jnp.float32)
+    qkv_sum = lax.psum(contract_rows(gathered_in, grad_packed), "dp")
+    grad_in_normed = lax.psum_scatter(
+        contract_cols(grad_packed, qkv_weight).astype(jnp.bfloat16),
+        "tensor",
+        scatter_dimension=0,
+        tiled=True,
+    ).astype(jnp.float32)
     grad_in_part, grad_in_gain = norm_back(grad_in_normed, in_unit, in_scale, in_gain)
     in_grad = grad_middle + grad_in_part
-    gains = lax.psum(
-        jnp.concatenate((grad_in_gain, grad_ffn_gain, grad_attn_gain, grad_hidden)),
-        ("dp", "tensor"),
-    )
+    gain_parts = jnp.concatenate((grad_in_gain, grad_ffn_gain, grad_attn_gain, grad_hidden))
+    sums, gains = grad_sync(
+        lax.axis_size("dp"),
+        rounded(grad_out),
+        rounded(grad_up.reshape(parts * width, -1)),
+        rounded(grad_down),
+        gain_parts.reshape(-1, 128),
+    )
+    gains = gains.reshape(-1)
     me = lax.axis_index("tensor")
     hidden = hidden_gain.shape[0]
+    sums = sums.reshape(-1, width).astype(jnp.float32)
+    down_sum, up_sum, out_sum = sums[:hidden], sums[hidden : hidden + width], sums[hidden + width :]
     return (
         result,
         in_grad,

time: 656 us -> 462 us (0.70)
  blocking collectives: 320 us -> 47.4 us
  Pallas kernels: 58.8 us -> 173 us
  waiting for transfers between devices: 124 us -> 78.8 us
  other arithmetic: 26.4 us -> 39.3 us
  matrix products: 78.9 us -> 69.1 us
    psum x2 -> x0, blocking collectives: 266 us -> none  [the longest x1 226 us: total(): return lax.psum(values, 'dp')]
    pallas_call x0 -> x1, Pallas kernels: none -> 115 us  [grad_sync(): pl.pallas_call(partial(sync_kernel, groups, sizes), out_shape=(jax.ShapeD...]
    reduce_scatter x4 -> x1, waiting for transfers between devices: 72.7 us -> 27.3 us  [local(): lax.psum_scatter(contract_cols(grad_packed, qkv_weight).astype(jnp.bfloat...]
    convert_element_type x1, other arithmetic: 9.83 us -> 22.3 us  [local(): gelu_pull(grad_act)[0].astype(jnp.bfloat16).reshape(own_rows, parts, -1)]
  transfers between devices with their start and end apart: 10 -> 7, of which waited for: 5 -> 3; matrix products, arithmetic and copies ran while one was open for 14% -> 16% of each run, Pallas kernels for 9% -> 30%
where the time goes in v3:
time: 462 us; the launch traced here: 453 us
  Pallas kernels  173 us (37%)
  waiting for transfers between devices  78.8 us (17%)
  matrix products  69.1 us (15%)
  blocking collectives  47.4 us (10%)
  other arithmetic  39.3 us (9%)
  local copies, waits for them, and re-layouts  26.1 us (6%)
  between operations  15.6 us (3%)
    pallas_call x1, Pallas kernels, grad_sync(): pl.pallas_call(partial(sync_kernel, groups, sizes), out_shape=(jax.ShapeD...  115 us
    all_gather x4, waiting for transfers between devices, gather(): return lax.all_gather(values, 'tensor', axis=0, tiled=True)  49.5 us
    pallas_call x1, Pallas kernels, attn_bwd(): pl.pallas_call(partial(bwd_kernel, bq, bk), out_shape=jax.ShapeDtypeStruc...  36.2 us
    unnamed x1, blocking collectives  29.4 us
    reduce_scatter x1, waiting for transfers between devices, local(): lax.psum_scatter(contract_cols(grad_packed, qkv_weight).astype(jnp.bfloat...  27.3 us
    pallas_call x1, Pallas kernels, attn_fwd(): pl.pallas_call(partial(fwd_kernel, bq, bk), out_shape=(jax.ShapeDtypeStru...  22.5 us
    convert_element_type x1, other arithmetic, local(): gelu_pull(grad_act)[0].astype(jnp.bfloat16).reshape(own_rows, parts, -1)  22.3 us
    all_to_all x1, blocking collectives, to_heads(): lax.all_to_all(blocks, 'tensor', 0, 0, tiled=True)  18 us
  transfers between devices with their start and end apart: 7, of which 3 were waited for; matrix products, arithmetic and copies ran while one was open for 16% of the time, Pallas kernels for 30%

profile of v3, /device:TPU:0, one launch (start us, length us, event | category | flops | bytes accessed | tf_op | source)
XLA Modules:
  0.0 453.5 jit_solution(7866426998790916452)
XLA Ops:
  7.2 1.7 convert_reduce_fusion
  8.9 2.5 fusion.27
  11.5 0.7 all-gather.7.cloned.1.call-update
  12.2 0.7 all-gather.9.cloned.1.call-update
  13.5 33.8 %all-gather.5.cloned.1.call-done = bf16[2560,768]{1,0:T(8,128)(2,1)} async-done(((bf16[640,768]{1,0:T(8,128)(2,1)}), bf16[2560,768]{1,0:T(8,128)(2,1)}) %all-gather.5.cloned.1.call-update) | async-done | bytes 3932176 | tf_op jit(solution)/shard_map/all_gather | solution.py:498
  47.3 5.4 %convolution_convert_fusion.2.qkv_ref = bf16[2560,576]{1,0:T(8,128)(2,1)S(1)} fusion(bf16[2560,768]{1,0:T(8,128)(2,1)} %all-gather.5.cloned.1.call-done, bf16[768,576]{0,1:T(8,128)(2,1)S(1)} %copy-done), kind=kOutput, calls=%fused_computation.18 | convolution fusion | flops 2266398720 | bytes 7766016 | tf_op jit(solution)/shard_map/dot_general | solution.py:517
  52.7 22.5 %attn_fwd.1 = (f32[2560,192]{1,0:T(8,128)S(1)}, f32[8,2560]{1,0:T(8,128)S(1)}) custom-call(s32[1,5]{1,0:T(1,128)S(1)} %copy-done.4, bf16[2560,576]{1,0:T(8,128)(2,1)S(1)} %convolution_convert_fusion.2.qkv_ref), custom_call_target="tpu_custom_call" | custom-call | tf_op jit(solution)/shard_map/attn_fwd/pallas_call | solution.py:143
  75.4 1.3 copy-done.2
  76.7 1.3 copy.28
  78.1 3.5 all-to-all-start
  81.7 0.6 dynamic-slice
  83.1 29.4 %all-reduce = f32[3840]{0:T(1024)S(1)} all-reduce(f32[3840]{0:T(1024)S(1)} %maximum_dynamic-update-slice_fusion), channel_id=1, replica_groups=mesh['dp'=8,'tensor'=4] {'tensor'}, use_global_device_ids=true, to_apply=%add | all-reduce | flops 3840 | bytes 30720
  112.8 1.6 convert_element_type.98
  114.4 1.9 copy.29
  116.2 1.5 convert_reduce_fusion.1
  117.8 3.9 fusion.37
  121.7 7.0 %copy.30 = bf16[4,768,768]{2,1,0:T(8,128)(2,1)} copy(bf16[4,768,768]{1,2,0:T(8,128)(2,1)} %bitcast.72) | data formatting | bytes 9437184 | tf_op jit(solution)/shard_map/rk,tkn->rtn/dot_general | solution.py:528
  128.7 10.5 %fusion.36 = (f32[640]{0:T(1024)S(1)}, f32[640]{0:T(1024)S(1)}, f32[640,3072]{1,0:T(8,128)}) fusion(bf16[3072,768]{1,0:T(8,128)(2,1)} %bitcast.75, f32[640,768]{1,0:T(8,128)} %get-tuple-element.52, f32[768]{0:T(1024)S(1)} %copy-done.22, f32[640]{0:T(1024)S(1)} %get-tuple-element.47, f32[640]{0:T(1024)S(1)} %get-tuple-element.46), kind=kOutput, calls=%fused_computation.90 | convolution fusion | flops 3043490816 | bytes 14562304 | tf_op jit(solution)/shard_map/rk,tkn->rtn/dot_general | solution.py:528
  139.2 15.7 %all-gather.11.cloned.1.call-done = bf16[3072,768]{1,0:T(8,128)(2,1)} async-done(((bf16[768,768]{1,0:T(8,128)(2,1)}), bf16[3072,768]{1,0:T(8,128)(2,1)}) %all-gather.11.cloned.1.call-update) | async-done | bytes 4718608 | tf_op jit(solution)/shard_map/all_gather | solution.py:498
  154.9 9.5 %multiply_reduce_fusion = (f32[3072]{0:T(1024)S(1)}, f32[640]{0:T(1024)S(1)}, f32[640]{0:T(1024)S(1)}, f32[640,3072]{1,0:T(8,128)S(1)}) fusion(f32[640]{0:T(1024)S(1)} %get-tuple-element.45, f32[640]{0:T(1024)S(1)} %get-tuple-element.44, f32[640,3072]{1,0:T(8,128)} %get-tuple-element.53, f32[3072]{0:T(1024)S(1)} %mul.295, bf16[640,768]{1,0:T(8,128)(2,1)} %param.21, ...), kind=kOutput, calls=%fused_computation.9 | convolution fusion | flops 3051352064 | bytes 21465088 | tf_op jit(solution)/shard_map/dot_general | solution.py:26
  164.5 22.3 %fusion.6 = (bf16[640,3072]{1,0:T(8,128)(2,1)S(1)}, bf16[640,3072]{1,0:T(8,128)(2,1)}) fusion(f32[640,3072]{1,0:T(8,128)S(1)} %bitcast.69, f32[640,3072]{1,0:T(8,128)S(1)} %get-tuple-element.54, f32[640]{0:T(1024)S(1)} %get-tuple-element.57, f32[640]{0:T(1024)S(1)} %get-tuple-element.58, f32[3072]{0:T(1024)S(1)} %mul.295, f32[640]{0:T(1024)S(1)} %get-tuple-element.45, ...), kind=kLoop, calls=%fused_computation.8 | loop fusion | flops 58982400 | bytes 23615488 | tf_op jit(solution)/shard_map/convert_element_type | solution.py:539
  186.8 7.4 %fusion.29 = (f32[768]{0:T(1024)S(1)}, f32[640]{0:T(1024)S(1)}, f32[640]{0:T(1024)S(1)}, f32[640,768,1]{1,0,2:T(8,128)S(1)}) fusion(f32[640,768]{1,0:T(8,128)S(1)} %copy-done.15, f32[640]{0:T(1024)S(1)} %get-tuple-element.47, f32[640]{0:T(1024)S(1)} %get-tuple-element.46, f32[768]{0:T(1024)S(1)} %copy-done.22, bf16[4,768,768]{2,1,0:T(8,128)(2,1)} %bitcast.73, ...), kind=kOutput, calls=%fused_computation.47 | convolution fusion | flops 3023828992 | bytes 12599296 | tf_op jit(solution)/shard_map/rtn,tkn->rk/dot_general | solution.py:541
  194.2 0.7 multiply_add_fusion
  195.0 0.5 copy-done.17
  195.5 1.3 multiply_reduce_fusion.4
  196.9 1.5 multiply_convert_fusion.1
  198.4 2.2 copy.32
  200.6 18.0 %all_to_all.10 = bf16[4,640,192]{1,2,0:T(8,128)(2,1)} all-to-all(bf16[4,640,192]{1,2,0:T(8,128)(2,1)} %bitcast.78), channel_id=1, replica_groups=mesh['dp'=8,'tensor'=4] {'tensor'}, dimensions={0} | all-to-all | bytes 1966080 | tf_op jit(solution)/shard_map/all_to_all | solution.py:507
  218.7 2.4 copy.33
  221.0 36.2 %attn_bwd.1 = bf16[2560,576]{1,0:T(8,128)(2,1)} custom-call(s32[1,5]{1,0:T(1,128)} %len_ref.3, bf16[2560,576]{1,0:T(8,128)(2,1)} %copy-done.1, f32[2560,192]{1,0:T(8,128)} %copy-done.2, f32[8,2560]{1,0:T(8,128)} %copy-done.3, bf16[2560,192]{1,0:T(8,128)(2,1)} %bitcast.71), custom_call_target="tpu_custom_call" | custom-call | tf_op jit(solution)/shard_map/attn_bwd/pallas_call | solution.py:248
  257.2 7.2 %convolution_convert_fusion.1 = bf16[2560,768]{1,0:T(8,128)(2,1)} fusion(bf16[2560,576]{1,0:T(8,128)(2,1)} %attn_bwd.1, bf16[768,576]{0,1:T(8,128)(2,1)S(1)} %copy-done), kind=kOutput, calls=%fused_computation.17 | convolution fusion | flops 2266890240 | bytes 7766016 | tf_op jit(solution)/shard_map/dot_general | solution.py:26
  264.5 4.1 convolution_convert_fusion.3.out_ref
  268.6 5.6 %convolution_convert_fusion.down_ref = bf16[3072,768]{1,0:T(8,128)(2,1)} fusion(bf16[640,3072]{1,0:T(8,128)(2,1)S(1)} %copy-done.11, bf16[640,768]{1,0:T(8,128)(2,1)S(1)} %copy-done.19), kind=kOutput, calls=%fused_computation.16 | convolution fusion | flops 3022258176 | bytes 9633792 | tf_op jit(solution)/shard_map/dot_general | solution.py:20
  274.2 6.2 %fusion.13 = bf16[4,768,768]{1,2,0:T(8,128)(2,1)} fusion(bf16[80,4,8,768]{3,2,1,0:T(8,128)(2,1)S(1)} %bitcast.77, f32[640,768]{1,0:T(8,128)S(1)} %copy-done.16, f32[768]{0:T(1024)S(1)} %copy-done.22, f32[640]{0:T(1024)S(1)} %get-tuple-element.47, f32[640]{0:T(1024)S(1)} %get-tuple-element.46), kind=kOutput, calls=%fused_computation.29 | convolution fusion | flops 3024224256 | bytes 10625024 | tf_op jit(solution)/shard_map/rk,rtn->tkn/dot_general | solution.py:540
  280.5 4.2 add_convert_fusion
  284.7 3.8 fusion.39
  288.5 27.3 %reduce-scatter.2.cloned.1.call-done = bf16[640,768]{1,0:T(8,128)(2,1)} async-done(((bf16[2560,768]{1,0:T(8,128)(2,1)}), bf16[640,768]{1,0:T(8,128)(2,1)}) %reduce-scatter.2.cloned.1.call-update) | async-done | bytes 983056 | tf_op jit(solution)/shard_map/reduce_scatter | solution.py:554
  315.9 2.2 fusion.23
  318.1 0.6 maximum_bitcast_fusion.gains_ref
  318.7 114.6 %grad_sync.1 = (bf16[9,192,768]{2,1,0:T(8,128)(2,1)}, f32[42,128]{1,0:T(8,128)}) custom-call(bf16[768,768]{1,0:T(8,128)(2,1)} %convolution_convert_fusion.3.out_ref, bf16[3072,768]{1,0:T(8,128)(2,1)} %bitcast.74, bf16[3072,768]{1,0:T(8,128)(2,1)} %convolution_convert_fusion.down_ref, f32[42,128]{1,0:T(8,128)} %maximum_bitcast_fusion.gains_ref), custom_call_target="tpu_custom_call" | custom-call | tf_op jit(solution)/shard_map/grad_sync/pallas_call | solution.py:443
  433.4 2.4 convert_element_type.96
  435.8 0.7 dynamic_slice.7
  436.5 0.6 dynamic_slice.6
  437.1 0.6 slice_bitcast_fusion.1
  437.7 0.9 slice_bitcast_fusion
  438.6 2.6 fusion.38
  441.5 2.0 fusion.21
  443.4 2.8 copy.54
  (95 shorter events, 1.9 us)
Async XLA Ops:
  7.2 40.1 %copy-start = (bf16[768,576]{0,1:T(8,128)(2,1)S(1)}, bf16[768,576]{0,1:T(8,128)(2,1)}, u32[]{:S(2)}) copy-start(bf16[768,576]{0,1:T(8,128)(2,1)} %param.14) | copy-start | bytes 2654212
  7.2 40.1 %all-gather.5.cloned.1.call-start = ((), (), s32[]{:S(2)}) async-start(), calls=%async_computation.3 | async-start | bytes 4915200 | tf_op jit(solution)/shard_map/all_gather | solution.py:498
  11.4 106.3 %all-gather.7.cloned.1.call-start = ((), (), s32[]{:S(2)}) async-start(), calls=%async_computation.4 | async-start | bytes 1474560 | tf_op jit(solution)/shard_map/all_gather | solution.py:498
  12.2 109.5 %all-gather.9.cloned.1.call-start = ((), (), s32[]{:S(2)}) async-start(), calls=%async_computation.5 | async-start | bytes 5898240 | tf_op jit(solution)/shard_map/all_gather | solution.py:498
  12.9 142.0 %all-gather.11.cloned.1.call-start = ((), (), s32[]{:S(2)}) async-start(), calls=%async_computation.6 | async-start | bytes 5898240 | tf_op jit(solution)/shard_map/all_gather | solution.py:498
  13.5 39.2 %copy-start.4 = (s32[1,5]{1,0:T(1,128)S(1)}, s32[1,5]{1,0:T(1,128)}, u32[]{:S(2)}) copy-start(s32[1,5]{1,0:T(1,128)} %len_ref.3) | copy-start | bytes 64
  52.7 22.7 %copy-start.1 = (bf16[2560,576]{1,0:T(8,128)(2,1)}, bf16[2560,576]{1,0:T(8,128)(2,1)S(1)}, u32[]{:S(2)}) copy-start(bf16[2560,576]{1,0:T(8,128)(2,1)S(1)} %convolution_convert_fusion.2.qkv_ref) | copy-start | bytes 8847364
  75.2 1.5 copy-start.2
  75.2 1.5 copy-start.3
  76.7 4.9 %copy-start.26 = (u32[32]{0:T(128)S(1)}, u32[32]{0:T(128)}, u32[]{:S(2)}) copy-start(u32[32]{0:T(128)} %constant.58) | copy-start | bytes 388
  76.7 6.2 %copy-start.23 = (f32[768]{0:T(1024)S(1)}, f32[768]{0:T(1024)}, u32[]{:S(2)}) copy-start(f32[768]{0:T(1024)} %param.19) | copy-start | bytes 9220
  76.7 6.2 %copy-start.24 = (f32[192]{0:T(256)S(1)}, f32[192]{0:T(256)}, u32[]{:S(2)}) copy-start(f32[192]{0:T(256)} %param.15) | copy-start | bytes 2308
  78.1 34.7 %all-to-all-start = ((bf16[4,640,192]{1,2,0:T(8,128)(2,1)}), bf16[4,640,192]{1,2,0:T(8,128)(2,1)S(1)}, u32[]{:S(2)}, u32[]{:S(2)}) async-start(bf16[4,640,192]{1,2,0:T(8,128)(2,1)} %copy.28), calls=%async_computation | async-start | bytes 1966080 | tf_op jit(solution)/shard_map/all_to_all | solution.py:502
  81.6 234.3 %reduce-scatter.2.cloned.1.call-start = ((), (), s32[]{:S(2)}) async-start(), calls=%async_computation.7 | async-start | bytes 4915200 | tf_op jit(solution)/shard_map/reduce_scatter | solution.py:554
  112.8 1.6 copy-start.9
  121.7 7.0 %copy-start.22 = (f32[768]{0:T(1024)S(1)}, f32[768]{0:T(1024)}, u32[]{:S(2)}) copy-start(f32[768]{0:T(1024)} %param.17) | copy-start | bytes 9220
  154.9 9.5 %slice-start = ((s8[7864320]{0:T(1024)(128)(4,1)}), s8[4194304]{0:T(1024)(128)(4,1)S(1)}, s32[]{:S(2)}) async-start(s8[7864320]{0:T(1024)(128)(4,1)} %bitcast.68), calls=%async_computation.9 | async-start | bytes 8388608
  154.9 9.5 %slice-start.1 = ((s8[7864320]{0:T(1024)(128)(4,1)}), s8[3670016]{0:T(1024)(128)(4,1)S(1)}, s32[]{:S(2)}) async-start(s8[7864320]{0:T(1024)(128)(4,1)} %bitcast.68), calls=%async_computation.10 | async-start | bytes 7340032
  164.5 22.3 %copy-start.15 = (f32[640,768]{1,0:T(8,128)S(1)}, f32[640,768]{1,0:T(8,128)}, u32[]{:S(2)}) copy-start(f32[640,768]{1,0:T(8,128)} %get-tuple-element.52) | copy-start | bytes 5898244
  186.8 7.4 %copy-start.12 = (bf16[640,3072]{1,0:T(8,128)(2,1)}, bf16[640,3072]{1,0:T(8,128)(2,1)S(1)}, u32[]{:S(2)}) copy-start(bf16[640,3072]{1,0:T(8,128)(2,1)S(1)} %get-tuple-element.38) | copy-start | bytes 11796484
  186.8 7.5 %copy-start.18 = (bf16[640,768]{1,0:T(8,128)(2,1)S(1)}, bf16[640,768]{1,0:T(8,128)(2,1)}, u32[]{:S(2)}) copy-start(bf16[640,768]{1,0:T(8,128)(2,1)} %param.21) | copy-start | bytes 2949124
  194.2 1.3 copy-start.17
  195.5 1.3 copy-start.6
  264.4 179.0 %all-reduce.3.cloned.1.call-start = ((), (), s32[]{:S(2)}) async-start(), calls=%async_computation.8 | async-start | bytes 3538944 | tf_op jit(solution)/shard_map/psum | solution.py:553
  264.5 4.1 copy-start.11
  264.5 4.1 copy-start.19
  264.5 16.0 %slice-start.2 = ((s8[4718592]{0:T(1024)(128)(4,1)}), s8[4194304]{0:T(1024)(128)(4,1)S(1)}, s32[]{:S(2)}) async-start(s8[4718592]{0:T(1024)(128)(4,1)} %bitcast.83), calls=%async_computation.11 | async-start | bytes 8388608
  268.6 5.7 %copy-start.13 = (bf16[640,3072]{1,0:T(8,128)(2,1)S(1)}, bf16[640,3072]{1,0:T(8,128)(2,1)}, u32[]{:S(2)}) copy-start(bf16[640,3072]{1,0:T(8,128)(2,1)} %copy-done.12) | copy-start | bytes 11796484
  268.6 5.7 %copy-start.16 = (f32[640,768]{1,0:T(8,128)S(1)}, f32[640,768]{1,0:T(8,128)}, u32[]{:S(2)}) copy-start(f32[640,768]{1,0:T(8,128)} %get-tuple-element.52) | copy-start | bytes 5898244
  268.6 11.9 %slice-start.3 = ((s8[4718592]{0:T(1024)(128)(4,1)}), s8[524288]{0:T(1024)(128)(4,1)S(1)}, s32[]{:S(2)}) async-start(s8[4718592]{0:T(1024)(128)(4,1)} %bitcast.83), calls=%async_computation.12 | async-start | bytes 1048576
  280.5 4.2 copy-start.14
  280.5 4.2 copy-start.25
  284.7 31.2 %copy-start.20 = (f32[768]{0:T(1024)S(1)}, f32[768]{0:T(1024)}, u32[]{:S(2)}) copy-start(f32[768]{0:T(1024)} %param.13) | copy-start | bytes 9220
  288.5 27.4 %copy-start.8 = (bf16[640,768]{1,0:T(8,128)(2,1)S(1)}, bf16[640,768]{1,0:T(8,128)(2,1)}, u32[]{:S(2)}) copy-start(bf16[640,768]{1,0:T(8,128)(2,1)} %param.11) | copy-start | bytes 2949124
  433.4 2.4 copy-start.21
  433.4 5.2 %copy-start.5 = (bf16[9,192,768]{2,1,0:T(8,128)(2,1)S(1)}, bf16[9,192,768]{2,1,0:T(8,128)(2,1)}, u32[]{:S(2)}) copy-start(bf16[9,192,768]{2,1,0:T(8,128)(2,1)} %get-tuple-element.17) | copy-start | bytes 7962628
  438.6 2.6 copy-start.7
  438.6 2.9 copy-start.10
Sparse Core Ops, SparseCore 0:
  11.6 35.6 all-gather.4
  48.8 17.4 all-gather.6
  67.9 48.2 all-gather.8
  117.6 37.2 all-gather.10
  264.5 51.2 reduce-scatter.1
  320.3 107.8 all-reduce.2

commit v4 on v3

--- a/solution.py
+++ b/solution.py
@@ -7,12 +7,8 @@
 from jax.experimental.pallas import tpu as pltpu
 from jax.sharding import PartitionSpec as P
 
-D = 768
 HEAD_DIM = 64
-FF = 3072
 UNIT = 64
-
-
 EPS = 1e-05
 
 
@@ -28,25 +24,9 @@
     )
 
 
-def normalize(values, gain):
-    row_mean = jnp.mean(values, axis=1, keepdims=True)
-    row_square = jnp.mean(values * values, axis=1, keepdims=True)
-    inv_scale = lax.rsqrt(row_square - row_mean * row_mean + EPS)
-    unit_rows = (values - row_mean) * inv_scale
-    return (unit_rows, inv_scale, unit_rows * gain)
-
-
-def norm_back(grad_normed, unit_rows, inv_scale, gain):
-    weighted = grad_normed * gain
-    first_mean = jnp.mean(weighted, axis=1, keepdims=True)
-    second = jnp.mean(weighted * unit_rows, axis=1, keepdims=True)
-    return (
-        inv_scale * (weighted - first_mean - unit_rows * second),
-        jnp.sum(grad_normed * unit_rows, axis=0),
-    )
-
-
 NEG = -1e30
+
+
 def seq_bounds(len_ref):
     ends, total = [], 0
     for s in range(len_ref.shape[1]):
@@ -309,24 +289,21 @@
     return values.astype(jnp.bfloat16)
 
 
-def sync_kernel(groups, sizes, out_ref, up_ref, down_ref, gains_ref, sum_ref, gains_sum_ref,
+def sync_kernel(groups, grads_ref, gains_ref, sum_ref, gains_sum_ref,
                 own, first, second, acc, to_y, to_x, from_x, to_z, from_z, to_w, from_w,
                 more_to, more_from, gain_at, send, recv, local_sem, gain_send, gain_recv):
     steps = peers_of(4, groups)
     me, dp = lax.axis_index("tensor"), lax.axis_index("dp")
-    cols = out_ref.shape[1]
+    cols = grads_ref.shape[2]
     half, rows2, rows4 = cols // 2, CHUNK // 2, CHUNK // 4
     b0, b1, b2 = dp % 2, (dp // 2) % 2, (dp // 4) % 2
-    chunks = []
-    for ref, size in zip((down_ref, up_ref, out_ref), sizes):
-        for at in range(0, size, CHUNK):
-            chunks.append((ref, size, at))
+    chunks = range(grads_ref.shape[1] // CHUNK)
     far = steps[5:]
     flight = {}
     sends = []
 
-    def take(ref, size, shard, at):
-        return ref.at[pl.ds(pl.multiple_of(shard * size + at, 16), CHUNK), :]
+    def take(c, shard):
+        return grads_ref.at[shard, pl.ds(c * CHUNK, CHUNK), :]
 
     def go(c, s, src, dst, axis, bit):
         copy = remote(src, dst, send.at[c, s], recv.at[c, s], axis, bit)
@@ -343,11 +320,10 @@
         return pl.ds(pl.multiple_of(b * rows2 + bb * rows4, 16), rows4)
 
     def pair(c):
-        ref, size, at = chunks[c]
-        go(c, 0, take(ref, size, flip(me, 1), at), first.at[c, 0], "tensor", 1)
-        go(c, 1, take(ref, size, flip(flip(me, 1), 2), at), first.at[c, 1], "tensor", 1)
+        go(c, 0, take(c, flip(me, 1)), first.at[c, 0], "tensor", 1)
+        go(c, 1, take(c, flip(flip(me, 1), 2)), first.at[c, 1], "tensor", 1)
         for k, shard in enumerate((me, flip(me, 2))):
-            copy = pltpu.make_async_copy(take(ref, size, shard, at), own.at[c, k], local_sem.at[c, k])
+            copy = pltpu.make_async_copy(take(c, shard), own.at[c, k], local_sem.at[c, k])
             copy.start()
             flight[c, "own", k] = copy
 
@@ -432,21 +408,20 @@
         copy.wait_send()
 
 
-def grad_sync(groups, grad_out, grad_up, grad_down, gains):
-    width = grad_out.shape[1]
-    sizes = tuple(g.shape[0] // 4 for g in (grad_down, grad_up, grad_out))
-    n = sum(sizes) // CHUNK
+def grad_sync(groups, grads, gains):
+    width = grads.shape[2]
+    n = grads.shape[1] // CHUNK
     steps = len(peers_of(4, groups))
     extra = max(steps - 5, 1)
     bf16 = lambda *shape: pltpu.VMEM(shape, jnp.bfloat16)
     anywhere, vmem = pl.BlockSpec(memory_space=pl.ANY), pl.BlockSpec(memory_space=pltpu.VMEM)
     return pl.pallas_call(
-        partial(sync_kernel, groups, sizes),
+        partial(sync_kernel, groups),
         out_shape=(
             jax.ShapeDtypeStruct((n, CHUNK, width), jnp.bfloat16),
             jax.ShapeDtypeStruct(gains.shape, jnp.float32),
         ),
-        in_specs=[anywhere] * 3 + [vmem],
+        in_specs=[anywhere, vmem],
         out_specs=[vmem, vmem],
         scratch_shapes=[
             bf16(n, 2, CHUNK, width),
@@ -473,7 +448,400 @@
             collective_id=0, has_side_effects=True, vmem_limit_bytes=56 << 20
         ),
         name="grad_sync",
-    )(grad_out, grad_up, grad_down, gains)
+    )(grads, gains)
+
+
+def spread(me):
+    return flip(me, 1), flip(me, 2), flip(flip(me, 1), 2)
+
+
+def greet_tensor(ids):
+    barrier = pltpu.get_barrier_semaphore()
+    for peer in ids:
+        pl.semaphore_signal(barrier, inc=1, device_id={"tensor": peer}, device_id_type=MESH)
+    pl.semaphore_wait(barrier, len(ids))
+
+
+def push(src, dst, send, recv, peer):
+    copy = pltpu.make_async_remote_copy(
+        src_ref=src,
+        dst_ref=dst,
+        send_sem=send,
+        recv_sem=recv,
+        device_id={"tensor": peer},
+        device_id_type=MESH,
+    )
+    copy.start()
+    return copy
+
+
+def intake_kernel(tok_ref, gain_ref, w_ref, own_gain_ref, all_ref, packed_ref, gains_ref,
+                  send, recv, gain_send, gain_recv):
+    me = lax.axis_index("tensor")
+    core, chip, cross = spread(me)
+    rows, width = tok_ref.shape
+    pieces = (send.shape[0] - 1) // 2
+    piece = rows // pieces
+    f32 = jnp.float32
+    values = tok_ref[...].astype(f32)
+    mu = jnp.sum(values, axis=1, keepdims=True) / width
+    ms = jnp.sum(values * values, axis=1, keepdims=True) / width
+    normed = (values - mu) * lax.rsqrt(ms - mu * mu + EPS) * gain_ref[...]
+    all_ref[me] = normed.astype(jnp.bfloat16)
+    gains_ref[me] = own_gain_ref[...]
+    greet_tensor((core, chip))
+
+    def span(c):
+        return pl.ds(c * piece, piece)
+
+    def block(c, owner):
+        return all_ref.at[owner, span(c), :]
+
+    to_chip = [push(block(c, me), block(c, me), send.at[c], recv.at[c], chip) for c in range(pieces)]
+    gain_chip = push(gains_ref.at[me], gains_ref.at[me], gain_send.at[0], gain_recv.at[0], chip)
+    to_core = push(all_ref.at[me], all_ref.at[me], send.at[2 * pieces], recv.at[2 * pieces], core)
+    gain_core = push(gains_ref.at[me], gains_ref.at[me], gain_send.at[1], gain_recv.at[1], core)
+
+    def project(owner, c):
+        product = jnp.dot(all_ref[owner, span(c), :], w_ref[...], preferred_element_type=f32)
+        packed_ref[owner, span(c), :] = product.astype(jnp.bfloat16)
+
+    for c in range(pieces):
+        project(me, c)
+    to_core.wait_recv()
+    for c in range(pieces):
+        project(core, c)
+    gain_chip.wait_recv()
+    gain_far = push(gains_ref.at[chip], gains_ref.at[chip], gain_send.at[2], gain_recv.at[2], core)
+    far = []
+    for c in range(pieces):
+        to_chip[c].wait_recv()
+        far.append(push(block(c, chip), block(c, chip), send.at[pieces + c], recv.at[pieces + c], core))
+        project(chip, c)
+    for c in range(pieces):
+        far[c].wait_recv()
+        project(cross, c)
+    gain_core.wait_recv()
+    gain_far.wait_recv()
+    for copy in [*to_chip, to_core, *far, gain_chip, gain_core, gain_far]:
+        copy.wait_send()
+
+
+def intake(tokens, gain, weight, own_gains, pieces=5):
+    rows, width = tokens.shape
+    vmem = pl.BlockSpec(memory_space=pltpu.VMEM)
+    return pl.pallas_call(
+        intake_kernel,
+        out_shape=(
+            jax.ShapeDtypeStruct((4, rows, width), jnp.bfloat16),
+            jax.ShapeDtypeStruct((4, rows, weight.shape[1]), jnp.bfloat16),
+            jax.ShapeDtypeStruct((4,) + own_gains.shape, jnp.float32),
+        ),
+        in_specs=[vmem] * 4,
+        out_specs=[vmem] * 3,
+        scratch_shapes=[
+            pltpu.SemaphoreType.DMA((2 * pieces + 1,)),
+            pltpu.SemaphoreType.DMA((2 * pieces + 1,)),
+            pltpu.SemaphoreType.DMA((3,)),
+            pltpu.SemaphoreType.DMA((3,)),
+        ],
+        compiler_params=pltpu.CompilerParams(
+            collective_id=1, has_side_effects=True, vmem_limit_bytes=40 << 20
+        ),
+        name="intake",
+    )(tokens, gain.reshape(1, -1), weight, own_gains)
+
+
+def exchange_kernel(in_ref, out_ref, send, recv, local_sem):
+    me = lax.axis_index("tensor")
+    peers = spread(me)
+    greet_tensor(peers)
+    moves = []
+    for n, peer in reversed(list(enumerate(peers))):
+        moves.append(push(in_ref.at[peer], out_ref.at[me], send.at[n], recv.at[n], peer))
+    own = pltpu.make_async_copy(in_ref.at[me], out_ref.at[me], local_sem)
+    own.start()
+    own.wait()
+    for move in moves:
+        move.wait()
+
+
+def exchange(blocks, number):
+    anywhere = pl.BlockSpec(memory_space=pltpu.VMEM)
+    return pl.pallas_call(
+        exchange_kernel,
+        out_shape=jax.ShapeDtypeStruct(blocks.shape, blocks.dtype),
+        in_specs=[anywhere],
+        out_specs=anywhere,
+        scratch_shapes=[
+            pltpu.SemaphoreType.DMA((3,)),
+            pltpu.SemaphoreType.DMA((3,)),
+            pltpu.SemaphoreType.DMA,
+        ],
+        compiler_params=pltpu.CompilerParams(
+            collective_id=number, has_side_effects=True, vmem_limit_bytes=24 << 20
+        ),
+        name="exchange",
+    )(blocks)
+
+
+def dot_nt(a, b):
+    return lax.dot_general(a, b, (((1,), (1,)), ((), ())), preferred_element_type=jnp.float32)
+
+
+def dot_tn(a, b):
+    return lax.dot_general(a, b, (((0,), (0,)), ((), ())), preferred_element_type=jnp.float32)
+
+
+GELU_A = 0.7978845608028654
+GELU_B = 0.044715
+
+
+def rows_kernel(tile, att_ref, tok_ref, og_ref, again_ref, fgain_ref, hgain_ref, wout_hbm, wup_hbm, wdown_hbm,
+                res_ref, gm_ref, datt_ref, g_hbm, gsum_ref,
+                wout, wup, wdown, x_s, mid_s, low_att, low_mid, act_s, slope_s, wide_s, low_act, big_s, acc_s,
+                mu_s, rs_s, mu4_s, rs4_s, one_s, two_s, stage, w_sem, g_sem):
+    parts, rows, head_width = att_ref.shape
+    width = tok_ref.shape[1]
+    hidden = width * hgain_ref.shape[0]
+    n_tiles = rows // tile
+    f32 = jnp.float32
+
+    loads = [pltpu.make_async_copy(wout_hbm, wout, w_sem.at[0])]
+    for t in range(parts):
+        loads.append(pltpu.make_async_copy(wup_hbm.at[t], wup.at[t], w_sem.at[1 + t]))
+    for t in range(parts):
+        loads.append(pltpu.make_async_copy(wdown_hbm.at[t], wdown.at[t], w_sem.at[1 + parts + t]))
+    for copy in loads:
+        copy.start()
+
+    def at(i):
+        return pl.ds(pl.multiple_of(i * tile, tile), tile)
+
+    def fold(v):
+        return jnp.sum(v.reshape(tile // 8, 8, width), axis=0)
+
+    def tiles(body, init=0):
+        return lax.fori_loop(0, n_tiles, body, init)
+
+    def stats(v, n):
+        mu = jnp.sum(v, axis=1, keepdims=True) / n
+        ms = jnp.sum(v * v, axis=1, keepdims=True) / n
+        return mu, lax.rsqrt(ms - mu * mu + EPS)
+
+    def save(slot, block, shard, row, n):
+        copy = pltpu.make_async_copy(
+            stage.at[slot, pl.ds(0, n), :], g_hbm.at[shard, pl.ds(row, n), :], g_sem.at[slot]
+        )
+        return copy
+
+    again = again_ref[...]
+    fgain = fgain_ref[...]
+
+    def first(i, _):
+        v = jnp.concatenate([att_ref[t, at(i), :] for t in range(parts)], axis=1).astype(f32)
+        x_s[at(i), :] = v
+        mu, rs = stats(v, width)
+        mu_s[at(i), :] = mu
+        rs_s[at(i), :] = rs
+        low_att[at(i), :] = ((v - mu) * rs * again).astype(jnp.bfloat16)
+        return 0
+
+    tiles(first)
+    loads[0].wait()
+    big_s[...] = jnp.dot(low_att[...], wout[...], preferred_element_type=f32)
+
+    def second(i, _):
+        v = tok_ref[at(i), :].astype(f32) + big_s[at(i), :]
+        mid_s[at(i), :] = v
+        mu, rs = stats(v, width)
+        low_mid[at(i), :] = ((v - mu) * rs * fgain).astype(jnp.bfloat16)
+        one_s[at(i), :] = jnp.zeros((tile, 1), f32)
+        two_s[at(i), :] = jnp.zeros((tile, 1), f32)
+        acc_s[at(i), :] = v
+        return 0
+
+    tiles(second)
+
+    for copy in loads[1:]:
+        copy.wait()
+
+    def up_block(t, _):
+        big_s[...] = jnp.dot(low_mid[...], wup[t], preferred_element_type=f32)
+
+        def body(i, _):
+            v = big_s[at(i), :]
+            sq = v * v
+            th = jnp.tanh(v * (GELU_A + (GELU_A * GELU_B) * sq))
+            half = 0.5 * th + 0.5
+            act = v * half
+            act_s[t, at(i), :] = act
+            slope = half + (0.5 * v) * (1.0 - th * th) * (GELU_A + (3.0 * GELU_A * GELU_B) * sq)
+            slope_s[t, at(i), :] = slope.astype(jnp.bfloat16)
+            one_s[at(i), :] += jnp.sum(act, axis=1, keepdims=True)
+            two_s[at(i), :] += jnp.sum(act * act, axis=1, keepdims=True)
+            return 0
+
+        tiles(body)
+        return 0
+
+    lax.fori_loop(0, parts, up_block, 0)
+
+    def third(i, _):
+        mu = one_s[at(i), :] / hidden
+        mu4_s[at(i), :] = mu
+        rs4_s[at(i), :] = lax.rsqrt(two_s[at(i), :] / hidden - mu * mu + EPS)
+        one_s[at(i), :] = jnp.zeros((tile, 1), f32)
+        two_s[at(i), :] = jnp.zeros((tile, 1), f32)
+        return 0
+
+    tiles(third)
+
+    def down_block(t, _):
+        hg = hgain_ref[t]
+        big_s[...] = dot_nt(og_ref[...], wdown[t])
+
+        def body(i, part):
+            unit = (act_s[t, at(i), :] - mu4_s[at(i), :]) * rs4_s[at(i), :]
+            act_s[t, at(i), :] = unit
+            low_act[at(i), :] = (unit * hg).astype(jnp.bfloat16)
+            d4 = big_s[at(i), :]
+            wide = d4 * hg
+            wide_s[t, at(i), :] = wide
+            one_s[at(i), :] += jnp.sum(wide, axis=1, keepdims=True)
+            two_s[at(i), :] += jnp.sum(wide * unit, axis=1, keepdims=True)
+            return part + fold(d4 * unit)
+
+        part = tiles(body, jnp.zeros((8, width), f32))
+        gsum_ref[pl.ds(2 + t, 1), :] = jnp.sum(part, axis=0, keepdims=True)
+        acc_s[...] += jnp.dot(low_act[...], wdown[t], preferred_element_type=f32)
+        slot = t % 2
+
+        @pl.when(t >= 2)
+        def _():
+            save(slot, None, t, 0, width).wait()
+
+        stage[slot] = dot_tn(low_act[...], og_ref[...]).astype(jnp.bfloat16)
+        save(slot, None, t, 0, width).start()
+        return 0
+
+    lax.fori_loop(0, parts, down_block, 0)
+
+    def fourth(i, _):
+        res_ref[at(i), :] = acc_s[at(i), :].astype(jnp.bfloat16)
+        one_s[at(i), :] = one_s[at(i), :] / hidden
+        two_s[at(i), :] = two_s[at(i), :] / hidden
+        acc_s[at(i), :] = jnp.zeros((tile, width), f32)
+        return 0
+
+    tiles(fourth)
+
+    def back_block(t, _):
+        def body(i, _):
+            d_act = rs4_s[at(i), :] * (wide_s[t, at(i), :] - one_s[at(i), :] - act_s[t, at(i), :] * two_s[at(i), :])
+            low_act[at(i), :] = (d_act * slope_s[t, at(i), :].astype(f32)).astype(jnp.bfloat16)
+            return 0
+
+        tiles(body)
+        acc_s[...] += dot_nt(low_act[...], wup[t])
+        slot = t % 2
+        save(slot, None, t, 0, width).wait()
+        stage[slot] = dot_tn(low_mid[...], low_act[...]).astype(jnp.bfloat16)
+        save(slot, None, t, width, width).start()
+        return 0
+
+    lax.fori_loop(0, parts, back_block, 0)
+
+    def fifth(i, part):
+        v = mid_s[at(i), :]
+        mu, rs = stats(v, width)
+        unit = (v - mu) * rs
+        d3 = acc_s[at(i), :]
+        wide = d3 * fgain
+        m1 = jnp.sum(wide, axis=1, keepdims=True) / width
+        m2 = jnp.sum(wide * unit, axis=1, keepdims=True) / width
+        d_mid = og_ref[at(i), :].astype(f32) + rs * (wide - m1 - unit * m2)
+        gm_ref[at(i), :] = d_mid
+        low_act[at(i), :] = d_mid.astype(jnp.bfloat16)
+        return part + fold(d3 * unit)
+
+    part = tiles(fifth, jnp.zeros((8, width), f32))
+    gsum_ref[0:1, :] = jnp.sum(part, axis=0, keepdims=True)
+    big_s[...] = dot_nt(low_act[...], wout[...])
+    for slot in range(2):
+        save(slot, None, slot, width, width).wait()
+    stage[0] = dot_tn(low_att[...], low_act[...]).astype(jnp.bfloat16)
+    last = []
+    for t in range(parts):
+        copy = pltpu.make_async_copy(
+            stage.at[0, pl.ds(t * head_width, head_width), :],
+            g_hbm.at[t, pl.ds(2 * width, head_width), :],
+            w_sem.at[t],
+        )
+        copy.start()
+        last.append(copy)
+
+    def sixth(i, part):
+        mu, rs = mu_s[at(i), :], rs_s[at(i), :]
+        unit = (x_s[at(i), :] - mu) * rs
+        d2 = big_s[at(i), :]
+        wide = d2 * again
+        m1 = jnp.sum(wide, axis=1, keepdims=True) / width
+        m2 = jnp.sum(wide * unit, axis=1, keepdims=True) / width
+        d_att = (rs * (wide - m1 - unit * m2)).astype(jnp.bfloat16)
+        for t in range(parts):
+            datt_ref[t, at(i), :] = d_att[:, t * head_width : (t + 1) * head_width]
+        return part + fold(d2 * unit)
+
+    part = tiles(sixth, jnp.zeros((8, width), f32))
+    gsum_ref[1:2, :] = jnp.sum(part, axis=0, keepdims=True)
+    gsum_ref[pl.ds(2 + parts, 8 - 2 - parts), :] = jnp.zeros((8 - 2 - parts, width), f32)
+    for copy in last:
+        copy.wait()
+
+
+def rows_pass(att, tokens, out_grad, attn_gain, ffn_gain, hidden_gain, w_out, w_up, w_down, tile=32):
+    parts, rows, head_width = att.shape
+    width = tokens.shape[1]
+    bf16, f32 = jnp.bfloat16, jnp.float32
+    vmem = pl.BlockSpec(memory_space=pltpu.VMEM)
+    anywhere = pl.BlockSpec(memory_space=pl.ANY)
+    column = pltpu.VMEM((rows, 1), f32)
+    return pl.pallas_call(
+        partial(rows_kernel, tile),
+        out_shape=(
+            jax.ShapeDtypeStruct((rows, width), bf16),
+            jax.ShapeDtypeStruct((rows, width), f32),
+            jax.ShapeDtypeStruct(att.shape, bf16),
+            jax.ShapeDtypeStruct((parts, 2 * width + head_width, width), bf16),
+            jax.ShapeDtypeStruct((8, width), f32),
+        ),
+        in_specs=[vmem] * 6 + [anywhere] * 3,
+        out_specs=[vmem] * 3 + [anywhere, vmem],
+        scratch_shapes=[
+            pltpu.VMEM((width, width), bf16),
+            pltpu.VMEM((parts, width, width), bf16),
+            pltpu.VMEM((parts, width, width), bf16),
+            pltpu.VMEM((rows, width), f32),
+            pltpu.VMEM((rows, width), f32),
+            pltpu.VMEM((rows, width), bf16),
+            pltpu.VMEM((rows, width), bf16),
+            pltpu.VMEM((parts, rows, width), f32),
+            pltpu.VMEM((parts, rows, width), bf16),
+            pltpu.VMEM((parts, rows, width), f32),
+            pltpu.VMEM((rows, width), bf16),
+            pltpu.VMEM((rows, width), f32),
+            pltpu.VMEM((rows, width), f32),
+        ] + [column] * 6 + [
+            pltpu.VMEM((2, width, width), bf16),
+            pltpu.SemaphoreType.DMA((1 + 2 * parts,)),
+            pltpu.SemaphoreType.DMA((2,)),
+        ],
+        compiler_params=pltpu.CompilerParams(vmem_limit_bytes=60 << 20),
+        cost_estimate=pl.CostEstimate(flops=20 * 10**9, bytes_accessed=40 << 20, transcendentals=2 * 10**6),
+        name="rows_pass",
+    )(att, tokens, out_grad, attn_gain.reshape(1, -1), ffn_gain.reshape(1, -1),
+      hidden_gain.reshape(parts, 1, -1), w_out, w_up, w_down)
 
 
 def local(
@@ -491,98 +859,73 @@
 ):
     parts = lax.axis_size("tensor")
     own_rows, width = tokens.shape
-    group_rows = own_rows * parts
-    head_width = attn_gain.shape[0]
+    head_width, hidden = attn_gain.shape[0], hidden_gain.shape[0]
 
     def gather(values):
-        return lax.all_gather(values, "tensor", axis=0, tiled=True)
-
-    def to_rows(values):
-        blocks = values.reshape(parts, own_rows, head_width)
-        moved = lax.all_to_all(blocks, "tensor", 0, 0, tiled=True)
-        return moved.transpose(1, 0, 2).reshape(own_rows, width)
-
-    def to_heads(values):
-        blocks = values.reshape(own_rows, parts, head_width).transpose(1, 0, 2)
-        return lax.all_to_all(blocks, "tensor", 0, 0, tiled=True).reshape(group_rows, head_width)
-
-    residual = tokens.astype(jnp.float32)
-    in_unit, in_scale, in_normed = normalize(residual, in_gain)
-    gathered_in = gather(in_normed.astype(jnp.bfloat16))
+        return lax.all_gather(values, "tensor", axis=0)
+
     full_out, full_up, full_down = gather(out_weight), gather(up_weight), gather(down_weight)
-    full_gains = gather(jnp.concatenate((attn_gain, hidden_gain))).reshape(parts, -1)
-    full_attn_gain = full_gains[:, :head_width].reshape(-1)
-    full_hidden_gain = full_gains[:, head_width:].reshape(-1)
-    full_up = full_up.reshape(parts, width, -1)
-    packed = jnp.dot(gathered_in, qkv_weight, preferred_element_type=jnp.float32).astype(
-        jnp.bfloat16
+    pad = -(head_width + hidden) % 1024
+    own_gains = jnp.concatenate((attn_gain, hidden_gain, jnp.zeros((pad,), jnp.float32)))
+    gathered_in, packed, gains = intake(tokens, in_gain, qkv_weight, own_gains.reshape(8, -1))
+    gathered_in = gathered_in.reshape(parts * own_rows, width)
+    packed = packed.reshape(parts * own_rows, -1)
+    gains = gains.reshape(parts, -1)
+    full_attn_gain = gains[:, :head_width].reshape(-1)
+    full_hidden_gain = gains[:, head_width : head_width + hidden].reshape(-1)
+
+    attended, log_total = attn_fwd(packed, lengths, 512, 512)
+    own_att = exchange(attended.astype(jnp.bfloat16).reshape(parts, own_rows, head_width), 2)
+    result, grad_middle, grad_att, grads, gain_parts = rows_pass(
+        own_att,
+        tokens,
+        out_grad,
+        full_attn_gain,
+        ffn_gain,
+        full_hidden_gain,
+        full_out.reshape(width, width),
+        full_up,
+        full_down,
+        own_rows,
     )
-    attended, log_total = attn_fwd(packed, lengths, 512, 512)
-    own_att = to_rows(attended.astype(jnp.bfloat16)).astype(jnp.float32)
-
-    att_unit, att_scale, att_normed = normalize(own_att, full_attn_gain)
-    att_low = att_normed.astype(jnp.bfloat16)
-    middle = residual + jnp.dot(att_low, full_out, preferred_element_type=jnp.float32)
-    mid_unit, mid_scale, mid_normed = normalize(middle, ffn_gain)
-    mid_low = mid_normed.astype(jnp.bfloat16)
-    pre_act = jnp.einsum("rk,tkn->rtn", mid_low, full_up, preferred_element_type=jnp.float32)
-    pre_act = pre_act.reshape(own_rows, -1)
-    activated, gelu_pull = jax.vjp(partial(jax.nn.gelu, approximate=True), pre_act)
-    act_unit, act_scale, act_normed = normalize(activated, full_hidden_gain)
-    act_low = act_normed.astype(jnp.bfloat16)
-    result = (middle + jnp.dot(act_low, full_down, preferred_element_type=jnp.float32)).astype(
-        jnp.bfloat16
-    )
-    grad_down = contract_rows(act_low, out_grad)
-    grad_act_low = contract_cols(out_grad, full_down)
-    grad_act, grad_hidden = norm_back(grad_act_low, act_unit, act_scale, full_hidden_gain)
-    grad_pre = gelu_pull(grad_act)[0].astype(jnp.bfloat16).reshape(own_rows, parts, -1)
-    grad_up = jnp.einsum("rk,rtn->tkn", mid_low, grad_pre, preferred_element_type=jnp.float32)
-    grad_mid_normed = jnp.einsum(
-        "rtn,tkn->rk", grad_pre, full_up, preferred_element_type=jnp.float32
-    )
-    grad_mid_part, grad_ffn_gain = norm_back(grad_mid_normed, mid_unit, mid_scale, ffn_gain)
-    grad_middle = out_grad.astype(jnp.float32) + grad_mid_part
-    grad_mid_low = grad_middle.astype(jnp.bfloat16)
-    grad_out = contract_rows(att_low, grad_mid_low)
-    grad_att_low = contract_cols(grad_mid_low, full_out)
-    grad_att, grad_attn_gain = norm_back(grad_att_low, att_unit, att_scale, full_attn_gain)
-    grad_attended = to_heads(grad_att.astype(jnp.bfloat16))
+    grad_attended = exchange(grad_att, 3).reshape(parts * own_rows, head_width)
 
     grad_packed = attn_bwd(packed, lengths, attended, log_total, grad_attended, 512, 256)
-    qkv_sum = lax.psum(contract_rows(gathered_in, grad_packed), "dp")
+    grad_qkv = contract_rows(gathered_in, grad_packed)
+    qkv_sum = lax.psum(grad_qkv, "dp")
     grad_in_normed = lax.psum_scatter(
         contract_cols(grad_packed, qkv_weight).astype(jnp.bfloat16),
         "tensor",
         scatter_dimension=0,
         tiled=True,
     ).astype(jnp.float32)
-    grad_in_part, grad_in_gain = norm_back(grad_in_normed, in_unit, in_scale, in_gain)
-    in_grad = grad_middle + grad_in_part
-    gain_parts = jnp.concatenate((grad_in_gain, grad_ffn_gain, grad_attn_gain, grad_hidden))
-    sums, gains = grad_sync(
-        lax.axis_size("dp"),
-        rounded(grad_out),
-        rounded(grad_up.reshape(parts * width, -1)),
-        rounded(grad_down),
-        gain_parts.reshape(-1, 128),
-    )
-    gains = gains.reshape(-1)
+    in_gain_part = jnp.sum(qkv_weight.astype(jnp.float32) * grad_qkv, axis=1) / in_gain
+    gain_parts = gain_parts.at[2 + parts].set(in_gain_part)
+    sums, gains = grad_sync(lax.axis_size("dp"), grads, gain_parts)
+
+    residual = tokens.astype(jnp.float32)
+    mean = jnp.mean(residual, axis=1, keepdims=True)
+    square = jnp.mean(residual * residual, axis=1, keepdims=True)
+    scale = lax.rsqrt(square - mean * mean + EPS)
+    unit = (residual - mean) * scale
+    weighted = grad_in_normed * in_gain
+    first = jnp.mean(weighted, axis=1, keepdims=True)
+    second = jnp.mean(weighted * unit, axis=1, keepdims=True)
+    in_grad = grad_middle + scale * (weighted - first - unit * second)
+
     me = lax.axis_index("tensor")
-    hidden = hidden_gain.shape[0]
     sums = sums.reshape(-1, width).astype(jnp.float32)
-    down_sum, up_sum, out_sum = sums[:hidden], sums[hidden : hidden + width], sums[hidden + width :]
     return (
         result,
         in_grad,
-        gains[:width],
+        gains[2 + parts],
         qkv_sum,
-        lax.dynamic_slice_in_dim(gains, 2 * width + me * head_width, head_width),
-        out_sum,
-        gains[width : 2 * width],
-        up_sum,
-        lax.dynamic_slice_in_dim(gains, 3 * width + me * hidden, hidden),
-        down_sum,
+        lax.dynamic_slice_in_dim(gains[1], me * head_width, head_width),
+        sums[hidden + width : hidden + width + head_width],
+        gains[0],
+        sums[hidden : hidden + width],
+        lax.dynamic_index_in_dim(gains, 2 + me, 0, keepdims=False),
+        sums[:hidden],
     )
 
 

time: 462 us -> 486 us (1.052)
  Pallas kernels: 173 us -> 320 us
  matrix products: 69.1 us -> 15 us
  blocking collectives: 47.4 us -> 0 us
  other arithmetic: 39.3 us -> 9.18 us
  waiting for transfers between devices: 78.8 us -> 95.6 us
    pallas_call x1 -> x5, Pallas kernels: 115 us -> 245 us  [the longest x1 119 us: grad_sync(): pl.pallas_call(partial(sync_kernel, groups), out_shape=(jax.ShapeDtypeStr...]
    psum x1, waiting for transfers between devices: 0.01 us -> 79.6 us  [local(): qkv_sum = lax.psum(grad_qkv, 'dp')]
    dot_general x6 -> x0, matrix products: 37.6 us -> none  [the longest x1 10.5 us: local(): jnp.einsum('rk,tkn->rtn', mid_low, full_up, preferred_element_type=jnp.fl...]
    all_gather x4 -> x3, waiting for transfers between devices: 49.5 us -> 13.9 us  [gather(): return lax.all_gather(values, 'tensor', axis=0)]
    unnamed x1 -> x0, blocking collectives: 29.4 us -> none
    convert_element_type x5 -> x1, other arithmetic: 28 us -> 0.13 us  [local(): attended.astype(jnp.bfloat16).reshape(parts, own_rows, head_width)]
    reduce_scatter x1, waiting for transfers between devices: 27.3 us -> 0.01 us  [local(): lax.psum_scatter(contract_cols(grad_packed, qkv_weight).astype(jnp.bfloat...]
    all_to_all x1 -> x0, blocking collectives: 18 us -> none  [to_heads(): lax.all_to_all(blocks, 'tensor', 0, 0, tiled=True)]
  transfers between devices with their start and end apart: 7 -> 5, of which waited for: 3 -> 2; matrix products, arithmetic and copies ran while one was open for 16% -> 6% of each run, Pallas kernels for 30% -> 45%
where the time goes in v4:
time: 486 us; the launch traced here: 477 us
  Pallas kernels  320 us (66%)
  waiting for transfers between devices  95.6 us (20%)
  local copies, waits for them, and re-layouts  21.9 us (5%)
  matrix products  15 us (3%)
  between operations  14.5 us (3%)
  other arithmetic  9.18 us (2%)
    pallas_call x1, Pallas kernels, grad_sync(): pl.pallas_call(partial(sync_kernel, groups), out_shape=(jax.ShapeDtypeStr...  119 us
    psum x1, waiting for transfers between devices, local(): qkv_sum = lax.psum(grad_qkv, 'dp')  79.6 us
    pallas_call x1, Pallas kernels, attn_bwd(): pl.pallas_call(partial(bwd_kernel, bq, bk), out_shape=jax.ShapeDtypeStruc...  45.7 us
    pallas_call x1, Pallas kernels, rows_pass(): pl.pallas_call(partial(rows_kernel, tile), out_shape=(jax.ShapeDtypeStruc...  45 us
    pallas_call x2, Pallas kernels, exchange(): pl.pallas_call(exchange_kernel, out_shape=jax.ShapeDtypeStruct(blocks.sha...  44.2 us
    pallas_call x1, Pallas kernels, intake(): pl.pallas_call(intake_kernel, out_shape=(jax.ShapeDtypeStruct((4, rows, w...  36.3 us
    pallas_call x1, Pallas kernels, attn_fwd(): pl.pallas_call(partial(fwd_kernel, bq, bk), out_shape=(jax.ShapeDtypeStru...  29.9 us
    all_gather x3, waiting for transfers between devices, gather(): return lax.all_gather(values, 'tensor', axis=0)  13.9 us
  transfers between devices with their start and end apart: 5, of which 2 were waited for; matrix products, arithmetic and copies ran while one was open for 6% of the time, Pallas kernels for 45%

profile of v4, /device:TPU:0, one launch (start us, length us, event | category | flops | bytes accessed | tf_op | source)
XLA Modules:
  0.0 477.2 jit_solution(14977921703054321913)
XLA Ops:
  7.2 0.0 all-gather.7.cloned.1.call-start
  7.2 0.7 all-gather.7.cloned.1.call-update
  8.0 0.0 copy-start
  8.0 0.0 all-gather.9.cloned.1.call-start
  8.0 0.7 all-gather.9.cloned.1.call-update
  8.7 0.0 all-gather.11.cloned.1.call-start
  8.8 0.7 all-gather.11.cloned.1.call-update
  9.4 0.0 copy-start.8
  9.5 0.0 reduce-scatter.2.cloned.1.call-start
  9.5 0.6 copy.21.w_ref
  10.2 0.1 maximum_bitcast_fusion.own_gain_ref
  10.3 36.3 %intake.1 = (bf16[4,640,768]{2,1,0:T(8,128)(2,1)S(1)}, bf16[4,640,576]{2,1,0:T(8,128)(2,1)S(1)}, f32[4,8,128]{2,1,0:T(8,128)S(1)}) custom-call(bf16[640,768]{1,0:T(8,128)(2,1)S(1)} %copy-done, f32[1,768]{1,0:T(1,128)S(1)} %reshape.107.gain_ref, bf16[768,576]{1,0:T(8,128)(2,1)S(1)} %copy.21.w_ref, f32[8,128]{1,0:T(8,128)S(1)} %maximum_bitcast_fusion.own_gain_ref), custom_call_target="tpu_custom_call" | custom-call | tf_op jit(solution)/shard_map/intake/pallas_call | solution.py:533
  46.6 1.9 copy-done.9
  48.5 0.1 slice.60
  48.6 29.9 %attn_fwd.1 = (f32[2560,192]{1,0:T(8,128)S(1)}, f32[8,2560]{1,0:T(8,128)S(1)}) custom-call(s32[1,5]{1,0:T(1,128)S(1)} %copy-done.8, bf16[2560,576]{1,0:T(8,128)(2,1)S(1)} %bitcast.21), custom_call_target="tpu_custom_call" | custom-call | tf_op jit(solution)/shard_map/attn_fwd/pallas_call | solution.py:123
  78.4 0.0 copy-start.7
  78.4 0.1 convert_element_type.19
  78.6 1.4 copy-done.3
  80.0 27.1 %exchange.2.att_ref = bf16[4,640,192]{2,1,0:T(8,128)(2,1)S(1)} custom-call(bf16[4,640,192]{2,1,0:T(8,128)(2,1)S(1)} %bitcast.23), custom_call_target="tpu_custom_call" | custom-call | tf_op jit(solution)/shard_map/exchange/pallas_call | solution.py:571
  107.1 0.0 copy-start.5
  107.1 1.0 copy-done.5
  108.2 0.6 reshape_reshape.7.hgain_ref
  108.8 0.7 reshape_reshape.6.again_ref
  109.4 0.6 reshape.112.fgain_ref
  110.0 13.9 %all-gather.11.cloned.1.call-done = bf16[3072,768]{1,0:T(8,128)(2,1)} async-done(((bf16[768,768]{1,0:T(8,128)(2,1)}), bf16[3072,768]{1,0:T(8,128)(2,1)}) %all-gather.11.cloned.1.call-update) | async-done | bytes 4718608 | tf_op jit(solution)/shard_map/all_gather | solution.py:865
  124.0 45.0 %rows_pass.1 = (bf16[640,768]{1,0:T(8,128)(2,1)}, f32[640,768]{1,0:T(8,128)}, bf16[4,640,192]{2,1,0:T(8,128)(2,1)}, bf16[4,1728,768]{2,1,0:T(8,128)(2,1)}, f32[8,768]{1,0:T(8,128)}) custom-call(bf16[4,640,192]{2,1,0:T(8,128)(2,1)} %copy-done.5, bf16[640,768]{1,0:T(8,128)(2,1)} %tok_ref.3, bf16[640,768]{1,0:T(8,128)(2,1)} %og_ref.1, ...), custom_call_target="tpu_custom_call" | custom-call | flops 20000000000 | bytes 41943040 | tf_op jit(solution)/shard_map/rows_pass/pallas_call | solution.py:810
  169.0 1.3 copy-done.6
  170.3 17.1 %exchange.3 = bf16[4,640,192]{2,1,0:T(8,128)(2,1)S(1)} custom-call(bf16[4,640,192]{2,1,0:T(8,128)(2,1)S(1)} %copy-done.6), custom_call_target="tpu_custom_call" | custom-call | tf_op jit(solution)/shard_map/exchange/pallas_call | solution.py:571
  187.4 1.0 copy-done.4
  188.5 45.7 %attn_bwd.1 = bf16[2560,576]{1,0:T(8,128)(2,1)} custom-call(s32[1,5]{1,0:T(1,128)} %len_ref.3, bf16[2560,576]{1,0:T(8,128)(2,1)} %bitcast.22, f32[2560,192]{1,0:T(8,128)} %copy-done.3, f32[8,2560]{1,0:T(8,128)} %copy-done.7, bf16[2560,192]{1,0:T(8,128)(2,1)} %bitcast.24), custom_call_target="tpu_custom_call" | custom-call | tf_op jit(solution)/shard_map/attn_bwd/pallas_call | solution.py:228
  234.2 7.2 %convolution_convert_fusion = bf16[2560,768]{1,0:T(8,128)(2,1)} fusion(bf16[2560,576]{1,0:T(8,128)(2,1)} %attn_bwd.1, bf16[768,576]{0,1:T(8,128)(2,1)S(1)} %copy-done.12), kind=kOutput, calls=%fused_computation | convolution fusion | flops 2266890240 | bytes 7766016 | tf_op jit(solution)/shard_map/dot_general | solution.py:22
  241.3 0.0 reduce-scatter.2.cloned.1.call-update
  241.3 0.3 all-reduce.2.cloned.1.call-start
  241.6 0.9 copy-done.1
  242.5 0.4 fusion
  242.9 7.8 %multiply_reduce_fusion = (f32[768]{0:T(1024)S(1)}, f32[768,576]{0,1:T(8,128)}) fusion(bf16[768,576]{0,1:T(8,128)(2,1)S(1)} %copy-done.12, bf16[2560,768]{1,0:T(8,128)(2,1)} %bitcast.26, bf16[2560,576]{1,0:T(8,128)(2,1)} %attn_bwd.1), kind=kOutput, calls=%fused_computation.14 | convolution fusion | flops 2266250496 | bytes 9538560 | tf_op jit(solution)/shard_map/dot_general | solution.py:16
  250.7 1.4 scatter.4.gains_ref
  252.1 119.5 %grad_sync.1 = (bf16[9,192,768]{2,1,0:T(8,128)(2,1)}, f32[8,768]{1,0:T(8,128)}) custom-call(bf16[4,1728,768]{2,1,0:T(8,128)(2,1)} %get-tuple-element.41.grads_ref, f32[8,768]{1,0:T(8,128)} %scatter.4.gains_ref), custom_call_target="tpu_custom_call" | custom-call | tf_op jit(solution)/shard_map/grad_sync/pallas_call | solution.py:418
  371.6 4.6 convert_element_type.24
  376.1 0.0 all-reduce.2.cloned.1.call-update
  376.2 0.6 dynamic-slice_reduce_fusion
  376.8 0.6 constant_dynamic-slice_fusion
  377.4 1.9 slice_bitcast_fusion
  379.3 4.4 fusion.9
  383.7 2.0 fusion.8
  385.8 2.0 fusion.7
  387.8 79.6 %all-reduce.2.cloned.1.call-done = f32[768,576]{0,1:T(8,128)} async-done(((f32[768,576]{0,1:T(8,128)}), f32[768,576]{0,1:T(8,128)}) %all-reduce.2.cloned.1.call-update) | async-done | bytes 1769488 | tf_op jit(solution)/shard_map/psum | solution.py:895
  467.4 2.8 copy.27
  (37 shorter events, 0.1 us)
Async XLA Ops:
  7.2 2.3 copy-start.12
  7.2 102.8 %all-gather.7.cloned.1.call-start = ((), (), s32[]{:S(2)}) async-start(), calls=%async_computation.3 | async-start | bytes 1474560 | tf_op jit(solution)/shard_map/all_gather | solution.py:865
  7.9 2.2 copy-start.13
  7.9 2.3 copy-start.16
  7.9 2.3 copy-start.17
  8.0 2.3 copy-start
  8.0 102.1 %all-gather.9.cloned.1.call-start = ((), (), s32[]{:S(2)}) async-start(), calls=%async_computation.4 | async-start | bytes 5898240 | tf_op jit(solution)/shard_map/all_gather | solution.py:865
  8.7 115.3 %all-gather.11.cloned.1.call-start = ((), (), s32[]{:S(2)}) async-start(), calls=%async_computation.5 | async-start | bytes 5898240 | tf_op jit(solution)/shard_map/all_gather | solution.py:865
  9.4 39.1 %copy-start.8 = (s32[1,5]{1,0:T(1,128)S(1)}, s32[1,5]{1,0:T(1,128)}, u32[]{:S(2)}) copy-start(s32[1,5]{1,0:T(1,128)} %len_ref.3) | copy-start | bytes 64
  9.5 374.3 %reduce-scatter.2.cloned.1.call-start = ((), (), s32[]{:S(2)}) async-start(), calls=%async_computation.1 | async-start | bytes 4915200 | tf_op jit(solution)/shard_map/reduce_scatter | solution.py:896
  46.6 1.9 copy-start.9
  48.5 30.1 %copy-start.2 = (bf16[4,640,576]{2,1,0:T(8,128)(2,1)}, bf16[4,640,576]{2,1,0:T(8,128)(2,1)S(1)}, u32[]{:S(2)}) copy-start(bf16[4,640,576]{2,1,0:T(8,128)(2,1)S(1)} %get-tuple-element.34) | copy-start | bytes 8847364
  78.4 1.6 copy-start.3
  78.4 1.6 copy-start.7
  80.0 29.5 %copy-start.15 = (f32[768]{0:T(1024)S(1)}, f32[768]{0:T(1024)}, u32[]{:S(2)}) copy-start(f32[768]{0:T(1024)} %param.19) | copy-start | bytes 9220
  107.1 1.1 copy-start.5
  169.0 1.3 copy-start.6
  187.4 1.1 copy-start.4
  241.3 1.2 copy-start.1
  241.3 226.1 %all-reduce.2.cloned.1.call-start = ((), (), s32[]{:S(2)}) async-start(), calls=%async_computation.2 | async-start | bytes 3538944 | tf_op jit(solution)/shard_map/psum | solution.py:895
  371.5 4.6 copy-start.14
  379.3 6.5 %copy-start.11 = (f32[640,768]{1,0:T(8,128)S(1)}, f32[640,768]{1,0:T(8,128)}, u32[]{:S(2)}) copy-start(f32[640,768]{1,0:T(8,128)} %get-tuple-element.38) | copy-start | bytes 5898244
  383.7 2.1 copy-start.10
Sparse Core Ops, SparseCore 0:
  9.6 26.5 all-gather.6
  37.8 37.4 all-gather.8
  76.8 47.0 all-gather.10
  241.5 56.3 reduce-scatter.1
  376.3 91.0 all-reduce.1
